TPU v7x, 256 devices: a whole 4x4x8 slice. The times are simulated.
256 devices in a mesh: tm: 32 (over y_hi, z, core), site: 8 (over y_lo, x).
Axes of the slice: x: 4, y: 4 (y_hi: 2, y_lo: 2; y = y_hi * 2 + y_lo), z: 8, core: 2. Of those that a mesh axis runs over, the one named last changes fastest.
Arguments:
- q_time: bfloat16 [8, 4096, 768], P('site', 'tm'), may hold values from -6 to 6
- k_time: bfloat16 [8, 4096, 768], P('site', 'tm'), may hold values from -6 to 6
- v_time: bfloat16 [8, 4096, 768], P('site', 'tm'), may hold values from -6 to 6
- resid: bfloat16 [8, 4096, 1536], P('site', 'tm'), may hold values from -6 to 6
- w_out_time: bfloat16 [768, 1536], replicated, may hold values from -0.21875 to 0.21875
- norm_gain: float32 [1536], replicated, may hold values from 0.1 to 1.9
- w_qkv_site: bfloat16 [1536, 2304], replicated, may hold values from -0.15625 to 0.15625
- grad_site: bfloat16 [8, 4096, 768], P('site', 'tm'), may hold values from -16 to 16
- nbr_blocks: int32 [8, 2], P('site'), may hold values from 0 to 7, as said below
Outputs:
- site_out: bfloat16 [8, 4096, 768], P('site', 'tm')
- grad_q_time: bfloat16 [8, 4096, 768], P('site', 'tm')
- grad_k_time: bfloat16 [8, 4096, 768], P('site', 'tm')
- grad_v_time: bfloat16 [8, 4096, 768], P('site', 'tm')
- grad_resid: bfloat16 [8, 4096, 1536], P('site', 'tm')
Inputs may be any that keep to these rules, and one draw needn't show every extreme that they name: `nbr_blocks`: each of a station's 2 entries names the station's own block or the block just below or just above it, station i lying in block i; in every block the first station names the block above first and the block below second, where these exist, and otherwise the one neighbouring block that exists.
All inputs are finite; a program needn't handle non-finite values.
Results may differ from a plain program's by a relative error of at most 0.017.
Values may be sent and summed in bfloat16 or wider, within the bound.
A program may use at most 64 MiB of HBM per device.

v0:
```python
import jax
import jax.numpy as jnp
from jax import lax
from jax.sharding import PartitionSpec as P

HEADS = 6
HEAD_SIZE = 128
RADIUS = 256


EPSILON = 1e-05


def passed_along(value, axis, steps):
    count = lax.axis_size(axis)
    initial, last = (max(0, -steps), min(count, count - steps))
    return lax.ppermute(value, axis, [(source, source + steps) for source in range(initial, last)])


def padded(cells, sides, width):
    for axis, dim in sides:
        count = lax.axis_size(axis)
        ends = count - 1
        head = lax.slice_in_dim(cells, 0, width, axis=dim)
        tail = lax.slice_in_dim(cells, cells.shape[dim] - width, cells.shape[dim], axis=dim)
        cells = jnp.concatenate(
            [
                lax.ppermute(tail, axis, [(i, (i + 1) % count) for i in range(ends)]),
                cells,
                lax.ppermute(head, axis, [((i + 1) % count, i) for i in range(ends)]),
            ],
            axis=dim,
        )
    return cells


def split_heads(values):
    return values.reshape(values.shape[:-1] + (HEADS, HEAD_SIZE))


def merge_heads(values):
    return values.reshape(values.shape[:-2] + (HEADS * HEAD_SIZE,))


def head_norm(values):
    shaped = split_heads(values)
    inverse = lax.rsqrt(jnp.mean(shaped * shaped, axis=-1, keepdims=True) + EPSILON)
    return (shaped * inverse, inverse)


def norm_back(normed, inverse, grads):
    return inverse * (grads - normed * jnp.mean(normed * grads, axis=-1, keepdims=True))


def shards(q_time, k_time, v_time, resid, w_out_time, norm_gain, w_qkv_site, grad_site, nbr_blocks):
    exact = lax.Precision.HIGHEST
    stations, hour_count, att_width = q_time.shape
    model_dim = resid.shape[2]
    row_count = stations * hour_count
    reach_count = (RADIUS + hour_count - 1) // hour_count
    window = 2 * reach_count + 1
    scale_factor = HEAD_SIZE ** (-0.5)
    tm_index = lax.axis_index("tm")
    tm_count = lax.axis_size("tm")
    site_index = lax.axis_index("site")
    packed = jnp.concatenate([k_time, v_time], axis=2)
    earlier_list = [passed_along(packed, "tm", offset) for offset in range(1, reach_count + 1)]
    later_list = [passed_along(packed, "tm", -offset) for offset in range(1, reach_count + 1)]
    key_window = jnp.concatenate(earlier_list[::-1] + [packed] + later_list, axis=1)
    k_window = key_window[:, :, :att_width]
    v_heads = split_heads(key_window[:, :, att_width:])
    key_rel = jnp.arange(window * hour_count, dtype=jnp.int32) - reach_count * hour_count
    key_shard = (
        tm_index + jnp.arange(window * hour_count, dtype=jnp.int32) // hour_count - reach_count
    )
    key_valid = (key_shard >= 0) & (key_shard < tm_count)
    query_rel = jnp.arange(hour_count, dtype=jnp.int32)
    in_band = (jnp.abs(query_rel[:, None] - key_rel[None, :]) <= RADIUS) & key_valid[None, :]
    qn_time, q_inverse = head_norm(q_time.astype(jnp.float32))
    kn_window, k_inverse = head_norm(k_window.astype(jnp.float32))
    scores = jnp.einsum("sqhe,skhe->shqk", qn_time, kn_window, precision=exact) * scale_factor
    exponent = jnp.where(in_band, jnp.exp(scores), 0.0)
    row_total = jnp.sum(exponent, axis=-1)
    prob_time = exponent / row_total[..., None]
    weights_time = prob_time.astype(jnp.bfloat16)
    out_time = jnp.einsum(
        "shqk,skhe->sqhe", weights_time, v_heads, preferred_element_type=jnp.float32
    ).astype(jnp.bfloat16)
    residual_sum = resid.reshape(row_count, model_dim).astype(jnp.float32) + jnp.dot(
        merge_heads(out_time).reshape(row_count, att_width),
        w_out_time,
        preferred_element_type=jnp.float32,
    )
    inv_rms = lax.rsqrt(jnp.mean(residual_sum * residual_sum, axis=1, keepdims=True) + EPSILON)
    normed = (residual_sum * inv_rms * norm_gain).astype(jnp.bfloat16)
    projected = jnp.dot(normed, w_qkv_site, preferred_element_type=jnp.float32)
    q_site = projected[:, :att_width].reshape(stations, hour_count, att_width)
    kv_site = (
        projected[:, att_width:].astype(jnp.bfloat16).reshape(stations, hour_count, 2 * att_width)
    )
    nearby = padded(kv_site, (("site", 0),), stations)
    k_near = nearby[:, :, :att_width]
    v_near = split_heads(nearby[:, :, att_width:])
    key_block = site_index - 1 + jnp.arange(3 * stations, dtype=jnp.int32) // stations
    allowed = (key_block[None, :] == site_index) | jnp.any(
        nbr_blocks[:, :, None] == key_block[None, None, :], axis=1
    )
    qn_site, qs_inverse = head_norm(q_site)
    kn_near, kn_inverse = head_norm(k_near.astype(jnp.float32))
    site_scores = jnp.einsum("ithe,jthe->thij", qn_site, kn_near, precision=exact) * scale_factor
    site_exponent = jnp.where(allowed, jnp.exp(site_scores), 0.0)
    prob_site = site_exponent / jnp.sum(site_exponent, axis=-1, keepdims=True)
    weights_site = prob_site.astype(jnp.bfloat16)
    site_heads = jnp.einsum(
        "thij,jthe->ithe", weights_site, v_near, preferred_element_type=jnp.float32
    )
    site_out = merge_heads(site_heads).astype(jnp.bfloat16)
    grad_heads = split_heads(grad_site)
    site_dprob = jnp.einsum(
        "ithe,jthe->thij", grad_heads, v_near, preferred_element_type=jnp.float32
    )
    site_dscore = prob_site * (site_dprob - jnp.sum(prob_site * site_dprob, axis=-1, keepdims=True))
    dq_site = norm_back(
        qn_site,
        qs_inverse,
        jnp.einsum("thij,jthe->ithe", site_dscore, kn_near, precision=exact) * scale_factor,
    )
    dk_near = norm_back(
        kn_near,
        kn_inverse,
        jnp.einsum("thij,ithe->jthe", site_dscore, qn_site, precision=exact) * scale_factor,
    )
    dv_near = jnp.einsum(
        "thij,ithe->jthe", weights_site, grad_heads, preferred_element_type=jnp.float32
    )
    near_grads = jnp.concatenate([merge_heads(dk_near), merge_heads(dv_near)], axis=2)
    from_upper = passed_along(near_grads[:stations].astype(jnp.bfloat16), "site", -1).astype(
        jnp.float32
    )
    from_lower = passed_along(near_grads[2 * stations :].astype(jnp.bfloat16), "site", 1).astype(
        jnp.float32
    )
    kv_grads = near_grads[stations : 2 * stations] + from_upper + from_lower
    d_projected = (
        jnp.concatenate([merge_heads(dq_site), kv_grads], axis=2)
        .astype(jnp.bfloat16)
        .reshape(row_count, 3 * att_width)
    )
    d_normed = lax.dot_general(
        d_projected, w_qkv_site, (((1,), (1,)), ((), ())), preferred_element_type=jnp.float32
    )
    gained = norm_gain * d_normed
    d_stream = inv_rms * gained - residual_sum * inv_rms * inv_rms * inv_rms * jnp.mean(
        residual_sum * gained, axis=1, keepdims=True
    )
    grad_resid = d_stream.astype(jnp.bfloat16)
    d_flat = lax.dot_general(
        grad_resid, w_out_time, (((1,), (1,)), ((), ())), preferred_element_type=jnp.float32
    ).astype(jnp.bfloat16)
    d_rows = d_flat.reshape(stations, hour_count, att_width)
    d_out = split_heads(d_rows)
    dprob_time = jnp.einsum("sqhe,skhe->shqk", d_out, v_heads, preferred_element_type=jnp.float32)
    delta_time = jnp.sum(prob_time * dprob_time, axis=-1)
    dscore_time = prob_time * (dprob_time - delta_time[..., None])
    grad_q_time = merge_heads(
        norm_back(
            qn_time,
            q_inverse,
            jnp.einsum("shqk,skhe->sqhe", dscore_time, kn_window, precision=exact) * scale_factor,
        )
    ).astype(jnp.bfloat16)
    dk_window = norm_back(
        kn_window,
        k_inverse,
        jnp.einsum("shqk,sqhe->skhe", dscore_time, qn_time, precision=exact) * scale_factor,
    )
    dv_window = jnp.einsum(
        "shqk,sqhe->skhe", weights_time, d_out, preferred_element_type=jnp.float32
    )
    window_grads = jnp.concatenate([merge_heads(dk_window), merge_heads(dv_window)], axis=2)

    def piece_of(position):
        return window_grads[:, position * hour_count : (position + 1) * hour_count]

    kv_total = piece_of(reach_count)
    for offset in range(1, reach_count + 1):
        early_part = piece_of(reach_count - offset)
        late_part = piece_of(reach_count + offset)
        kv_total = kv_total + passed_along(early_part.astype(jnp.bfloat16), "tm", -offset).astype(
            early_part.dtype
        )
        kv_total = kv_total + passed_along(late_part.astype(jnp.bfloat16), "tm", offset).astype(
            late_part.dtype
        )
    grad_k_time = kv_total[:, :, :att_width].astype(jnp.bfloat16)
    grad_v_time = kv_total[:, :, att_width:].astype(jnp.bfloat16)
    return (
        site_out,
        grad_q_time,
        grad_k_time,
        grad_v_time,
        grad_resid.reshape(stations, hour_count, model_dim),
    )


def solution(mesh):
    placed = (
        P("site", "tm", None),
        P("site", "tm", None),
        P("site", "tm", None),
        P("site", "tm", None),
        P(),
        P(),
        P(),
        P("site", "tm", None),
        P("site", None),
    )
    return jax.shard_map(
        shards,
        mesh=mesh,
        in_specs=placed,
        out_specs=(
            P("site", "tm", None),
            P("site", "tm", None),
            P("site", "tm", None),
            P("site", "tm", None),
            P("site", "tm", None),
        ),
        check_vma=False,
    )
```

profile of v0, /device:TPU:24, one launch (start us, length us, event | category | flops | bytes accessed | tf_op | source)
XLA Modules:
  0.0 159.0 jit_solution(11379532644136995453)
XLA Ops:
  0.7 1.2 copy.46
  1.9 1.1 copy.47
  3.0 0.8 pad_maximum_fusion.3
  3.8 8.4 %collective-permute-start.3 = (bf16[1,128,1536]{1,2,0:T(8,128)(2,1)}, bf16[1,128,1536]{1,2,0:T(8,128)(2,1)}, u32[]{:S(2)}, u32[]{:S(2)}) collective-permute-start(bf16[1,128,1536]{1,2,0:T(8,128)(2,1)} %pad_maximum_fusion.3), channel_id=1, source_target_pairs={{16,0},{24,8},{32,16},{40,24},{48,32},{56,40},{64,48},{72,56},{80,... | collective-permute-start | bytes 1179656 | tf_op jit(solution)/shard_map/ppermute | solution.py:17
  12.2 2.1 %collective-permute-start.2 = (bf16[1,128,1536]{1,2,0:T(8,128)(2,1)}, bf16[1,128,1536]{1,2,0:T(8,128)(2,1)}, u32[]{:S(2)}, u32[]{:S(2)}) collective-permute-start(bf16[1,128,1536]{1,2,0:T(8,128)(2,1)} %pad_maximum_fusion.3), channel_id=1, source_target_pairs={{8,0},{16,8},{24,16},{32,24},{40,32},{48,40},{56,48},{64,56},{72,6... | collective-permute-start | bytes 1179656 | tf_op jit(solution)/shard_map/ppermute | solution.py:17
  14.3 2.3 %collective-permute-start.1 = (bf16[1,128,1536]{1,2,0:T(8,128)(2,1)}, bf16[1,128,1536]{1,2,0:T(8,128)(2,1)}, u32[]{:S(2)}, u32[]{:S(2)}) collective-permute-start(bf16[1,128,1536]{1,2,0:T(8,128)(2,1)} %pad_maximum_fusion.3), channel_id=1, source_target_pairs={{0,8},{8,16},{16,24},{24,32},{32,40},{40,48},{48,56},{56,64},{64,7... | collective-permute-start | bytes 1179656 | tf_op jit(solution)/shard_map/ppermute | solution.py:17
  16.6 2.6 %collective-permute-start = (bf16[1,128,1536]{1,2,0:T(8,128)(2,1)}, bf16[1,128,1536]{1,2,0:T(8,128)(2,1)}, u32[]{:S(2)}, u32[]{:S(2)}) collective-permute-start(bf16[1,128,1536]{1,2,0:T(8,128)(2,1)} %pad_maximum_fusion.3), channel_id=1, source_target_pairs={{0,16},{8,24},{16,32},{24,40},{32,48},{40,56},{48,64},{56,72},{64,... | collective-permute-start | bytes 1179656 | tf_op jit(solution)/shard_map/ppermute | solution.py:17
  19.7 1.1 copy.48
  21.1 0.8 convert.44
  21.9 0.7 compare_reduce_fusion
  23.3 11.1 %collective-permute-done = bf16[1,128,1536]{1,2,0:T(8,128)(2,1)} collective-permute-done((bf16[1,128,1536]{1,2,0:T(8,128)(2,1)}, bf16[1,128,1536]{1,2,0:T(8,128)(2,1)}, u32[]{:S(2)}, u32[]{:S(2)}) %collective-permute-start) | collective-permute-done | bytes 393248 | tf_op jit(solution)/shard_map/ppermute | solution.py:17
  34.4 1.1 constant_dynamic-update-slice_fusion.4
  35.5 1.1 constant_dynamic-update-slice_fusion.3
  36.7 1.1 constant_dynamic-update-slice_fusion.1
  37.8 1.1 constant_dynamic-update-slice_fusion
  39.4 2.3 %fusion.9 = (f32[6,128]{1,0:T(8,128)S(1)}, f32[6,128,640]{2,1,0:T(8,128)S(1)}) fusion(pred[128,640]{1,0:T(8,128)(4,1)S(1)} %fusion.44, f32[640,6,128]{0,2,1:T(8,128)S(1)} %bitcast.84, f32[640,6]{0,1:T(8,128)S(1)} %add_rsqrt_fusion, f32[128,6,128]{0,2,1:T(8,128)S(1)} %bitcast.98, f32[128,6]{0,1:T(8,128)S(1)} %add_rsqrt_fusion.3), kind=kOutput, calls=%fused_computation.23 | convolution fusion | flops 757038336 | bytes 4428800 | tf_op jit(solution)/shard_map/sqhe,skhe->shqk/dot_general | solution.py:81
  41.7 0.7 convolution_convert_fusion
  43.0 0.6 multiply_reduce_fusion.8
  43.6 1.4 slice-done.1
  45.1 1.2 fusion.37
  46.3 0.8 slice_multiply_fusion
  47.1 3.9 %collective-permute-start.5 = (bf16[1,128,1536]{2,1,0:T(8,128)(2,1)S(1)}, bf16[1,128,1536]{2,1,0:T(8,128)(2,1)}, u32[]{:S(2)}, u32[]{:S(2)}) collective-permute-start(bf16[1,128,1536]{2,1,0:T(8,128)(2,1)S(1)} %fusion.38), channel_id=1, source_target_pairs={{1,0},{2,1},{3,2},{4,3},{5,4},{6,5},{7,6},{9,8},{10,9},{11,10},{12... | collective-permute-start | bytes 1179656 | tf_op jit(solution)/shard_map/ppermute | solution.py:30
  51.1 1.9 %collective-permute-start.4 = (bf16[1,128,1536]{2,1,0:T(8,128)(2,1)S(1)}, bf16[1,128,1536]{2,1,0:T(8,128)(2,1)}, u32[]{:S(2)}, u32[]{:S(2)}) collective-permute-start(bf16[1,128,1536]{2,1,0:T(8,128)(2,1)S(1)} %fusion.38), channel_id=1, source_target_pairs={{0,1},{1,2},{2,3},{3,4},{4,5},{5,6},{6,7},{8,9},{9,10},{10,11},{11... | collective-permute-start | bytes 1179656 | tf_op jit(solution)/shard_map/ppermute | solution.py:28
  53.2 1.2 copy.52
  54.4 0.8 broadcast_multiply_fusion.1
  55.2 5.7 %collective-permute-done.5 = bf16[1,128,1536]{2,1,0:T(8,128)(2,1)} collective-permute-done((bf16[1,128,1536]{2,1,0:T(8,128)(2,1)S(1)}, bf16[1,128,1536]{2,1,0:T(8,128)(2,1)}, u32[]{:S(2)}, u32[]{:S(2)}) %collective-permute-start.5) | collective-permute-done | bytes 393248 | tf_op jit(solution)/shard_map/ppermute | solution.py:30
  61.0 6.1 %collective-permute-done.4 = bf16[1,128,1536]{2,1,0:T(8,128)(2,1)} collective-permute-done((bf16[1,128,1536]{2,1,0:T(8,128)(2,1)S(1)}, bf16[1,128,1536]{2,1,0:T(8,128)(2,1)}, u32[]{:S(2)}, u32[]{:S(2)}) %collective-permute-start.4) | collective-permute-done | bytes 393248 | tf_op jit(solution)/shard_map/ppermute | solution.py:28
  67.1 1.2 pad_maximum_fusion.2
  68.3 1.3 slice_convert_fusion.2
  69.6 1.6 %copy.54 = f32[3,128,768]{1,2,0:T(8,128)S(1)} copy(f32[3,128,768]{2,1,0:T(8,128)} %get-tuple-element.30) | data formatting | bytes 2359296 | tf_op jit(solution)/shard_map/reshape | solution.py:38
  71.4 2.1 %copy.89 = bf16[3,128,768]{1,2,0:T(8,128)(2,1)} copy(bf16[3,128,768]{2,1,0:T(8,128)(2,1)} %get-tuple-element.31) | data formatting | bytes 1179648
  73.5 1.7 %multiply_reduce_fusion.3 = (f32[128,6,3]{0,1,2:T(8,128)S(1)}, f32[128,6,3]{0,1,2:T(8,128)S(1)}) fusion(bf16[128,6,128,3]{0,2,1,3:T(8,128)(2,1)} %bitcast.105, f32[128,6,128]{0,2,1:T(8,128)} %convert.44, f32[3,128,6,128]{1,3,2,0:T(8,128)S(1)} %bitcast.79, f32[3,128,6]{1,2,0:T(8,128)S(1)} %add_rsqrt_fusion.1, f32[128,6,128]{0,2,1:T(8,128)} %broadcast_multiply_fusion.1), kind=kLoop, calls=%fused_computation.32 | loop fusion | flops 1764864 | bytes 2583552 | tf_op jit(solution)/shard_map/ithe,jthe->thij/dot_general | solution.py:119
  75.7 0.9 multiply_reduce_fusion.2
  76.6 0.6 broadcast_multiply_fusion.3
  77.2 1.9 %broadcast_multiply_fusion = (f32[128,6,3,128]{0,3,1,2:T(8,128)}, bf16[128,6,128]{0,2,1:T(8,128)(2,1)}) fusion(f32[128,6,3]{0,1,2:T(8,128)S(1)} %get-tuple-element.35, f32[128,6,128]{0,2,1:T(8,128)S(1)} %copy-done.12, bf16[128,6,3,128]{0,3,1,2:T(8,128)(2,1)S(1)} %bitcast.106), kind=kLoop, calls=%fused_computation.62 | loop fusion | flops 1081344 | bytes 2368512 | tf_op jit(solution)/shard_map/thij,ithe->jthe/dot_general | solution.py:133
  79.1 1.7 %copy.61 = bf16[1,128,768]{2,1,0:T(8,128)(2,1)} copy(bf16[1,128,768]{1,2,0:T(8,128)(2,1)} %bitcast.112) | data formatting | bytes 393216
  80.9 1.4 fusion.17
  82.3 1.2 multiply_reduce_fusion.10
  83.5 1.6 fusion.1
  85.1 2.1 %collective-permute-start.6 = (bf16[1,128,1536]{1,2,0:T(8,128)(2,1)S(1)}, bf16[1,128,1536]{1,2,0:T(8,128)(2,1)S(1)}, u32[]{:S(2)}, u32[]{:S(2)}) collective-permute-start(bf16[1,128,1536]{1,2,0:T(8,128)(2,1)S(1)} %get-tuple-element.26), channel_id=1, source_target_pairs={{1,0},{2,1},{3,2},{4,3},{5,4},{6,5},{7,6},{9,8},{10,9},{11,10},{12... | collective-permute-start | bytes 1179656 | tf_op jit(solution)/shard_map/ppermute | solution.py:17
  87.2 4.1 %collective-permute-start.7 = (bf16[1,128,1536]{1,2,0:T(8,128)(2,1)S(1)}, bf16[1,128,1536]{1,2,0:T(8,128)(2,1)S(1)}, u32[]{:S(2)}, u32[]{:S(2)}) collective-permute-start(bf16[1,128,1536]{1,2,0:T(8,128)(2,1)S(1)} %get-tuple-element.27), channel_id=1, source_target_pairs={{0,1},{1,2},{2,3},{3,4},{4,5},{5,6},{6,7},{8,9},{9,10},{10,11},{11... | collective-permute-start | bytes 1179656 | tf_op jit(solution)/shard_map/ppermute | solution.py:17
  91.5 6.7 %collective-permute-done.6 = bf16[1,128,1536]{1,2,0:T(8,128)(2,1)S(1)} collective-permute-done((bf16[1,128,1536]{1,2,0:T(8,128)(2,1)S(1)}, bf16[1,128,1536]{1,2,0:T(8,128)(2,1)S(1)}, u32[]{:S(2)}, u32[]{:S(2)}) %collective-permute-start.6) | collective-permute-done | bytes 393248 | tf_op jit(solution)/shard_map/ppermute | solution.py:17
  98.2 4.0 %collective-permute-done.7 = bf16[1,128,1536]{1,2,0:T(8,128)(2,1)S(1)} collective-permute-done((bf16[1,128,1536]{1,2,0:T(8,128)(2,1)S(1)}, bf16[1,128,1536]{1,2,0:T(8,128)(2,1)S(1)}, u32[]{:S(2)}, u32[]{:S(2)}) %collective-permute-start.7) | collective-permute-done | bytes 393248 | tf_op jit(solution)/shard_map/ppermute | solution.py:17
  102.4 2.5 %multiply_reduce_fusion.7 = (f32[128]{0:T(128)S(1)}, f32[128,1536]{1,0:T(8,128)S(1)}) fusion(f32[128,1536]{1,0:T(8,128)S(1)} %copy-done.4, bf16[1536,2304]{1,0:T(8,128)(2,1)S(1)} %bitcast.91, bf16[128,1536]{0,1:T(8,128)(2,1)S(1)} %fusion.41, bf16[128,768]{0,1:T(8,128)(2,1)S(1)} %bitcast.115, f32[1536]{0:T(1024)S(1)} %copy-done.29), kind=kOutput, calls=%fused_computation.54 | convolution fusion | flops 907739008 | bytes 9247232 | tf_op jit(solution)/shard_map/dot_general | solution.py:149
  105.2 0.9 convolution_convert_fusion.1
  106.3 2.8 %multiply_reduce_fusion = (f32[6,128]{1,0:T(8,128)S(1)}, f32[6,128,640]{2,1,0:T(8,128)S(1)}) fusion(f32[6,128]{1,0:T(8,128)S(1)} %copy-done.32, f32[6,128,640]{2,1,0:T(8,128)} %copy-done.14, pred[128,640]{1,0:T(8,128)(4,1)S(1)} %copy-done.21, bf16[128,6,128]{0,2,1:T(8,128)(2,1)S(1)} %bitcast.117, bf16[640,6,128]{0,2,1:T(8,128)(2,1)} %bitcast.111), kind=kOutput, calls=%fused_computation.15 | convolution fusion | flops 128285952 | bytes 5199872 | tf_op jit(solution)/shard_map/sqhe,skhe->shqk/dot_general | solution.py:162
  109.4 3.8 %multiply_reduce_fusion.9 = (f32[128,6]{0,1:T(8,128)S(1)}, f32[1,128,6,128]{1,3,2,0:T(8,128)}) fusion(f32[1,128,6,128]{1,3,2,0:T(8,128)S(1)} %bitcast.99, f32[128,6]{0,1:T(8,128)S(1)} %copy-done.27, f32[6,128,640]{2,1,0:T(8,128)S(1)} %get-tuple-element.45, f32[6,128]{1,0:T(8,128)S(1)} %get-tuple-element.44, f32[6,128]{1,0:T(8,128)S(1)} %copy-done.32, ...), kind=kOutput, calls=%fused_computation.70 | convolution fusion | flops 758316288 | bytes 6794240 | tf_op jit(solution)/shard_map/shqk,skhe->sqhe/dot_general | solution.py:169
  113.2 3.9 %fusion.2 = (f32[640,6]{0,1:T(8,128)S(1)}, f32[6,128,640]{2,1,0:T(8,128)}) fusion(f32[1,640,6,128]{1,3,2,0:T(8,128)S(1)} %bitcast.87, f32[640,6]{0,1:T(8,128)S(1)} %copy-done.25, f32[6,128,640]{2,1,0:T(8,128)S(1)} %get-tuple-element.45, f32[6,128]{1,0:T(8,128)S(1)} %get-tuple-element.44, f32[6,128]{1,0:T(8,128)S(1)} %copy-done.32, ...), kind=kOutput, calls=%fused_computation.12 | convolution fusion | flops 759492864 | bytes 8379392 | tf_op jit(solution)/shard_map/shqk,sqhe->skhe/dot_general | solution.py:175
  117.1 2.0 %fusion.34 = f32[6,128,640]{2,1,0:T(8,128)} fusion(bf16[128,6,128]{0,2,1:T(8,128)(2,1)S(1)} %bitcast.118, f32[6,128,640]{2,1,0:T(8,128)S(1)} %copy-done.15, f32[6,128]{1,0:T(8,128)S(1)} %copy-done.32, pred[128,640]{1,0:T(8,128)(4,1)S(1)} %copy-done.21), kind=kOutput, calls=%fused_computation.63 | convolution fusion | flops 127795200 | bytes 4213760 | tf_op jit(solution)/shard_map/shqk,sqhe->skhe/dot_general | solution.py:177
  119.1 2.9 %copy.60 = f32[1,640,768]{2,1,0:T(8,128)} copy(f32[1,640,768]{1,2,0:T(8,128)} %bitcast.107) | data formatting | bytes 3932160 | tf_op jit(solution)/shard_map/reshape | solution.py:42
  121.9 3.7 %fusion.3 = f32[1,640,6,128]{1,3,2,0:T(8,128)} fusion(f32[1,640,6,128]{1,3,2,0:T(8,128)} %bitcast.85, f32[6,128,640]{2,1,0:T(8,128)} %get-tuple-element.49, f32[640,6]{0,1:T(8,128)S(1)} %broadcast_multiply_fusion.2, f32[640,6]{0,1:T(8,128)S(1)} %copy-done.25), kind=kLoop, calls=%fused_computation.13 | loop fusion | flops 2457600 | bytes 5928960 | tf_op jit(solution)/shard_map/mul | solution.py:52
  125.7 2.9 %copy.59 = f32[1,640,768]{2,1,0:T(8,128)} copy(f32[1,640,768]{1,2,0:T(8,128)} %bitcast.96) | data formatting | bytes 3932160 | tf_op jit(solution)/shard_map/reshape | solution.py:42
  128.6 2.4 %fusion = bf16[1,640,1536]{2,1,0:T(8,128)(2,1)S(1)} fusion(f32[1,640,768]{2,1,0:T(8,128)} %copy.60, f32[1,640,768]{2,1,0:T(8,128)} %copy.59), kind=kLoop, calls=%fused_computation.3 | loop fusion | flops 3932160 | bytes 5898240 | tf_op jit(solution)/shard_map/convert.9
  130.9 1.2 fusion.62
  132.2 1.9 %collective-permute-start.8 = (bf16[1,128,1536]{2,1,0:T(8,128)(2,1)}, bf16[1,128,1536]{2,1,0:T(8,128)(2,1)S(1)}, u32[]{:S(2)}, u32[]{:S(2)}) collective-permute-start(bf16[1,128,1536]{2,1,0:T(8,128)(2,1)} %get-tuple-element.20), channel_id=1, source_target_pairs={{8,0},{16,8},{24,16},{32,24},{40,32},{48,40},{56,48},{64,56},{72,6... | collective-permute-start | bytes 1179656 | tf_op jit(solution)/shard_map/ppermute | solution.py:17
  134.1 2.7 %collective-permute-start.11 = (bf16[1,128,1536]{2,1,0:T(8,128)(2,1)}, bf16[1,128,1536]{2,1,0:T(8,128)(2,1)}, u32[]{:S(2)}, u32[]{:S(2)}) collective-permute-start(bf16[1,128,1536]{2,1,0:T(8,128)(2,1)} %get-tuple-element.21), channel_id=1, source_target_pairs={{0,16},{8,24},{16,32},{24,40},{32,48},{40,56},{48,64},{56,72},{64,... | collective-permute-start | bytes 1179656 | tf_op jit(solution)/shard_map/ppermute | solution.py:17
  136.8 6.8 %collective-permute-start.10 = (bf16[1,128,1536]{2,1,0:T(8,128)(2,1)}, bf16[1,128,1536]{2,1,0:T(8,128)(2,1)}, u32[]{:S(2)}, u32[]{:S(2)}) collective-permute-start(bf16[1,128,1536]{2,1,0:T(8,128)(2,1)} %get-tuple-element.22), channel_id=1, source_target_pairs={{16,0},{24,8},{32,16},{40,24},{48,32},{56,40},{64,48},{72,56},{80,... | collective-permute-start | bytes 1179656 | tf_op jit(solution)/shard_map/ppermute | solution.py:17
  143.6 1.9 %collective-permute-start.9 = (bf16[1,128,1536]{2,1,0:T(8,128)(2,1)}, bf16[1,128,1536]{2,1,0:T(8,128)(2,1)}, u32[]{:S(2)}, u32[]{:S(2)}) collective-permute-start(bf16[1,128,1536]{2,1,0:T(8,128)(2,1)} %get-tuple-element.23), channel_id=1, source_target_pairs={{0,8},{8,16},{16,24},{24,32},{32,40},{40,48},{48,56},{56,64},{64,7... | collective-permute-start | bytes 1179656 | tf_op jit(solution)/shard_map/ppermute | solution.py:17
  145.6 0.8 copy.62
  146.4 5.0 %collective-permute-done.11 = bf16[1,128,1536]{2,1,0:T(8,128)(2,1)} collective-permute-done((bf16[1,128,1536]{2,1,0:T(8,128)(2,1)}, bf16[1,128,1536]{2,1,0:T(8,128)(2,1)}, u32[]{:S(2)}, u32[]{:S(2)}) %collective-permute-start.11) | collective-permute-done | bytes 393248 | tf_op jit(solution)/shard_map/ppermute | solution.py:17
  151.4 1.2 collective-permute-done.10
  152.6 4.0 %collective-permute-done.9 = bf16[1,128,1536]{2,1,0:T(8,128)(2,1)} collective-permute-done((bf16[1,128,1536]{2,1,0:T(8,128)(2,1)}, bf16[1,128,1536]{2,1,0:T(8,128)(2,1)}, u32[]{:S(2)}, u32[]{:S(2)}) %collective-permute-start.9) | collective-permute-done | bytes 393248 | tf_op jit(solution)/shard_map/ppermute | solution.py:17
  156.6 1.7 %fusion.29 = bf16[1,128,1536]{2,1,0:T(8,128)(2,1)S(1)} fusion(f32[1,640,768]{2,1,0:T(8,128)} %copy.59, f32[1,640,768]{2,1,0:T(8,128)} %copy.60, bf16[1,128,1536]{2,1,0:T(8,128)(2,1)} %collective-permute-done.11, bf16[1,128,1536]{2,1,0:T(8,128)(2,1)} %collective-permute-done.10, bf16[1,128,1536]{2,1,0:T(8,128)(2,1)} %collective-permute-done.9, ...), kind=kLoop, calls=%fused_computation.51 | loop fusion | flops 1966080 | bytes 5898240 | tf_op jit(solution)/shard_map/convert.5
  158.3 0.8 fusion.64
  (119 shorter events, 4.4 us)
Async XLA Ops:
  0.6 42.3 %copy-start = (bf16[768,1536]{1,0:T(8,128)(2,1)S(1)}, bf16[768,1536]{1,0:T(8,128)(2,1)}, u32[]{:S(2)}) copy-start(bf16[768,1536]{1,0:T(8,128)(2,1)} %param.13) | copy-start | bytes 7077892
  0.6 20.3 %copy-start.23 = (bf16[1,128,768]{2,1,0:T(8,128)(2,1)S(1)}, bf16[1,128,768]{2,1,0:T(8,128)(2,1)}, u32[]{:S(2)}) copy-start(bf16[1,128,768]{2,1,0:T(8,128)(2,1)} %param.16) | copy-start | bytes 589828
  0.7 21.2 %copy-start.35 = (s32[1,2]{1,0:T(1,128)S(1)}, s32[1,2]{1,0:T(1,128)}, u32[]{:S(2)}) copy-start(s32[1,2]{1,0:T(1,128)} %param.17) | copy-start | bytes 28
  3.8 34.0 %collective-permute-start.3 = (bf16[1,128,1536]{1,2,0:T(8,128)(2,1)}, bf16[1,128,1536]{1,2,0:T(8,128)(2,1)}, u32[]{:S(2)}, u32[]{:S(2)}) collective-permute-start(bf16[1,128,1536]{1,2,0:T(8,128)(2,1)} %pad_maximum_fusion.3), channel_id=1, source_target_pairs={{16,0},{24,8},{32,16},{40,24},{48,32},{56,40},{64,48},{72,56},{80,... | collective-permute-start | bytes 1179656 | tf_op jit(solution)/shard_map/ppermute | solution.py:17
  12.2 24.5 %collective-permute-start.2 = (bf16[1,128,1536]{1,2,0:T(8,128)(2,1)}, bf16[1,128,1536]{1,2,0:T(8,128)(2,1)}, u32[]{:S(2)}, u32[]{:S(2)}) collective-permute-start(bf16[1,128,1536]{1,2,0:T(8,128)(2,1)} %pad_maximum_fusion.3), channel_id=1, source_target_pairs={{8,0},{16,8},{24,16},{32,24},{40,32},{48,40},{56,48},{64,56},{72,6... | collective-permute-start | bytes 1179656 | tf_op jit(solution)/shard_map/ppermute | solution.py:17
  14.3 21.2 %collective-permute-start.1 = (bf16[1,128,1536]{1,2,0:T(8,128)(2,1)}, bf16[1,128,1536]{1,2,0:T(8,128)(2,1)}, u32[]{:S(2)}, u32[]{:S(2)}) collective-permute-start(bf16[1,128,1536]{1,2,0:T(8,128)(2,1)} %pad_maximum_fusion.3), channel_id=1, source_target_pairs={{0,8},{8,16},{16,24},{24,32},{32,40},{40,48},{48,56},{56,64},{64,7... | collective-permute-start | bytes 1179656 | tf_op jit(solution)/shard_map/ppermute | solution.py:17
  16.6 17.9 %collective-permute-start = (bf16[1,128,1536]{1,2,0:T(8,128)(2,1)}, bf16[1,128,1536]{1,2,0:T(8,128)(2,1)}, u32[]{:S(2)}, u32[]{:S(2)}) collective-permute-start(bf16[1,128,1536]{1,2,0:T(8,128)(2,1)} %pad_maximum_fusion.3), channel_id=1, source_target_pairs={{0,16},{8,24},{16,32},{24,40},{32,48},{40,56},{48,64},{56,72},{64,... | collective-permute-start | bytes 1179656 | tf_op jit(solution)/shard_map/ppermute | solution.py:17
  20.8 18.5 %copy-start.6 = (f32[1,128,768]{1,2,0:T(8,128)}, f32[1,128,768]{1,2,0:T(8,128)S(1)}, u32[]{:S(2)}) copy-start(f32[1,128,768]{1,2,0:T(8,128)S(1)} %convert_element_type.100) | copy-start | bytes 1179652
  22.7 18.9 %copy-start.20 = (pred[128,640]{1,0:T(8,128)(4,1)}, pred[128,640]{1,0:T(8,128)(4,1)S(1)}, u32[]{:S(2)}) copy-start(pred[128,640]{1,0:T(8,128)(4,1)S(1)} %fusion.44) | copy-start | bytes 245764
  22.8 16.6 %copy-start.26 = (f32[128,6]{0,1:T(8,128)}, f32[128,6]{0,1:T(8,128)S(1)}, u32[]{:S(2)}) copy-start(f32[128,6]{0,1:T(8,128)S(1)} %add_rsqrt_fusion.3) | copy-start | bytes 9220
  39.1 2.5 %copy-start.1 = (f32[1,640,768]{1,2,0:T(8,128)}, f32[1,640,768]{1,2,0:T(8,128)S(1)}, u32[]{:S(2)}) copy-start(f32[1,640,768]{1,2,0:T(8,128)S(1)} %get-tuple-element.24) | copy-start | bytes 5898244
  39.1 2.6 %copy-start.17 = (bf16[1,640,768]{1,2,0:T(8,128)(2,1)}, bf16[1,640,768]{1,2,0:T(8,128)(2,1)S(1)}, u32[]{:S(2)}) copy-start(bf16[1,640,768]{1,2,0:T(8,128)(2,1)S(1)} %get-tuple-element.25) | copy-start | bytes 2949124
  39.3 2.3 %copy-start.24 = (f32[640,6]{0,1:T(8,128)}, f32[640,6]{0,1:T(8,128)S(1)}, u32[]{:S(2)}) copy-start(f32[640,6]{0,1:T(8,128)S(1)} %add_rsqrt_fusion) | copy-start | bytes 46084
  39.4 4.2 %slice-start = ((s8[7077888]{0:T(1024)(128)(4,1)}), s8[2883584]{0:T(1024)(128)(4,1)S(1)}, s32[]{:S(2)}) async-start(s8[7077888]{0:T(1024)(128)(4,1)} %bitcast.88), calls=%async_computation | async-start | bytes 5767168
  41.7 1.3 copy-start.14
  41.7 1.3 copy-start.31
  41.7 1.3 copy-start.19
  41.7 3.3 %slice-start.1 = ((s8[7077888]{0:T(1024)(128)(4,1)}), s8[4194304]{0:T(1024)(128)(4,1)S(1)}, s32[]{:S(2)}) async-start(s8[7077888]{0:T(1024)(128)(4,1)} %bitcast.88), calls=%async_computation.1 | async-start | bytes 8388608
  42.9 2.1 %copy-start.28 = (f32[1536]{0:T(1024)S(1)}, f32[1536]{0:T(1024)}, u32[]{:S(2)}) copy-start(f32[1536]{0:T(1024)} %param.14) | copy-start | bytes 18436
  43.6 2.7 %copy-start.3 = (f32[128,1536]{1,0:T(8,128)}, f32[128,1536]{1,0:T(8,128)S(1)}, u32[]{:S(2)}) copy-start(f32[128,1536]{1,0:T(8,128)S(1)} %get-tuple-element.41) | copy-start | bytes 2359300
  43.6 2.7 %copy-start.33 = (f32[128]{0:T(128)}, f32[128]{0:T(128)S(1)}, u32[]{:S(2)}) copy-start(f32[128]{0:T(128)S(1)} %add_rsqrt_fusion.4) | copy-start | bytes 1540
  47.1 13.8 %collective-permute-start.5 = (bf16[1,128,1536]{2,1,0:T(8,128)(2,1)S(1)}, bf16[1,128,1536]{2,1,0:T(8,128)(2,1)}, u32[]{:S(2)}, u32[]{:S(2)}) collective-permute-start(bf16[1,128,1536]{2,1,0:T(8,128)(2,1)S(1)} %fusion.38), channel_id=1, source_target_pairs={{1,0},{2,1},{3,2},{4,3},{5,4},{6,5},{7,6},{9,8},{10,9},{11,10},{12... | collective-permute-start | bytes 1179656 | tf_op jit(solution)/shard_map/ppermute | solution.py:30
  51.1 16.0 %collective-permute-start.4 = (bf16[1,128,1536]{2,1,0:T(8,128)(2,1)S(1)}, bf16[1,128,1536]{2,1,0:T(8,128)(2,1)}, u32[]{:S(2)}, u32[]{:S(2)}) collective-permute-start(bf16[1,128,1536]{2,1,0:T(8,128)(2,1)S(1)} %fusion.38), channel_id=1, source_target_pairs={{0,1},{1,2},{2,3},{3,4},{4,5},{5,6},{6,7},{8,9},{9,10},{10,11},{11... | collective-permute-start | bytes 1179656 | tf_op jit(solution)/shard_map/ppermute | solution.py:28
  54.3 15.3 %copy-start.8 = (f32[128,768]{0,1:T(8,128)}, f32[128,768]{0,1:T(8,128)S(1)}, u32[]{:S(2)}) copy-start(f32[128,768]{0,1:T(8,128)S(1)} %copy.52) | copy-start | bytes 1179652
  73.5 1.7 %copy-start.30 = (pred[3]{0:T(512)(128)(4,1)S(1)}, pred[3]{0:T(512)(128)(4,1)}, u32[]{:S(2)}) copy-start(pred[3]{0:T(512)(128)(4,1)} %compare_or_fusion) | copy-start | bytes 13
  73.5 1.9 %copy-start.10 = (f32[128,6,128]{0,2,1:T(8,128)S(1)}, f32[128,6,128]{0,2,1:T(8,128)}, u32[]{:S(2)}) copy-start(f32[128,6,128]{0,2,1:T(8,128)} %broadcast_multiply_fusion.1) | copy-start | bytes 1179652
  75.2 2.0 %copy-start.11 = (bf16[3,128,768]{1,2,0:T(8,128)(2,1)S(1)}, bf16[3,128,768]{1,2,0:T(8,128)(2,1)}, u32[]{:S(2)}) copy-start(bf16[3,128,768]{1,2,0:T(8,128)(2,1)} %copy.89) | copy-start | bytes 1769476
  75.2 2.0 %copy-start.12 = (f32[128,6,128]{0,2,1:T(8,128)S(1)}, f32[128,6,128]{0,2,1:T(8,128)}, u32[]{:S(2)}) copy-start(f32[128,6,128]{0,2,1:T(8,128)} %convert.44) | copy-start | bytes 1179652
  75.4 3.7 %copy-start.22 = (f32[128,6,3]{0,1,2:T(8,128)}, f32[128,6,3]{0,1,2:T(8,128)S(1)}, u32[]{:S(2)}) copy-start(f32[128,6,3]{0,1,2:T(8,128)S(1)} %get-tuple-element.34) | copy-start | bytes 27652
  80.9 21.5 %slice-start.2 = ((s8[7077888]{0:T(1024)(128)(4,1)}), s8[4194304]{0:T(1024)(128)(4,1)S(1)}, s32[]{:S(2)}) async-start(s8[7077888]{0:T(1024)(128)(4,1)} %bitcast.90), calls=%async_computation.2 | async-start | bytes 8388608
  83.5 7.9 %copy-start.9 = (f32[128,768]{0,1:T(8,128)S(1)}, f32[128,768]{0,1:T(8,128)}, u32[]{:S(2)}) copy-start(f32[128,768]{0,1:T(8,128)} %copy-done.8) | copy-start | bytes 1179652
  83.5 7.9 %copy-start.13 = (f32[128,6,128]{0,2,1:T(8,128)S(1)}, f32[128,6,128]{0,2,1:T(8,128)}, u32[]{:S(2)}) copy-start(f32[128,6,128]{0,2,1:T(8,128)} %multiply_reduce_fusion.2) | copy-start | bytes 1179652
  83.5 18.9 %slice-start.3 = ((s8[7077888]{0:T(1024)(128)(4,1)}), s8[2883584]{0:T(1024)(128)(4,1)S(1)}, s32[]{:S(2)}) async-start(s8[7077888]{0:T(1024)(128)(4,1)} %bitcast.90), calls=%async_computation.3 | async-start | bytes 5767168
  85.1 17.1 %copy-start.5 = (f32[128,6,3,128]{0,3,1,2:T(8,128)S(1)}, f32[128,6,3,128]{0,3,1,2:T(8,128)}, u32[]{:S(2)}) copy-start(f32[128,6,3,128]{0,3,1,2:T(8,128)} %get-tuple-element.36) | copy-start | bytes 3538948
  85.1 13.0 %collective-permute-start.6 = (bf16[1,128,1536]{1,2,0:T(8,128)(2,1)S(1)}, bf16[1,128,1536]{1,2,0:T(8,128)(2,1)S(1)}, u32[]{:S(2)}, u32[]{:S(2)}) collective-permute-start(bf16[1,128,1536]{1,2,0:T(8,128)(2,1)S(1)} %get-tuple-element.26), channel_id=1, source_target_pairs={{1,0},{2,1},{3,2},{4,3},{5,4},{6,5},{7,6},{9,8},{10,9},{11,10},{12... | collective-permute-start | bytes 1179656 | tf_op jit(solution)/shard_map/ppermute | solution.py:17
  87.2 15.0 %collective-permute-start.7 = (bf16[1,128,1536]{1,2,0:T(8,128)(2,1)S(1)}, bf16[1,128,1536]{1,2,0:T(8,128)(2,1)S(1)}, u32[]{:S(2)}, u32[]{:S(2)}) collective-permute-start(bf16[1,128,1536]{1,2,0:T(8,128)(2,1)S(1)} %get-tuple-element.27), channel_id=1, source_target_pairs={{0,1},{1,2},{2,3},{3,4},{4,5},{5,6},{6,7},{8,9},{9,10},{10,11},{11... | collective-permute-start | bytes 1179656 | tf_op jit(solution)/shard_map/ppermute | solution.py:17
  91.4 10.9 %copy-start.4 = (f32[128,1536]{1,0:T(8,128)S(1)}, f32[128,1536]{1,0:T(8,128)}, u32[]{:S(2)}) copy-start(f32[128,1536]{1,0:T(8,128)} %copy-done.3) | copy-start | bytes 2359300
  91.5 10.9 %copy-start.29 = (f32[1536]{0:T(1024)S(1)}, f32[1536]{0:T(1024)}, u32[]{:S(2)}) copy-start(f32[1536]{0:T(1024)} %param.14) | copy-start | bytes 18436
  102.4 2.5 %copy-start.34 = (f32[128]{0:T(128)S(1)}, f32[128]{0:T(128)}, u32[]{:S(2)}) copy-start(f32[128]{0:T(128)} %copy-done.33) | copy-start | bytes 1540
  105.2 4.0 %copy-start.16 = (bf16[128,1536]{1,0:T(8,128)(2,1)}, bf16[128,1536]{1,0:T(8,128)(2,1)S(1)}, u32[]{:S(2)}) copy-start(bf16[128,1536]{1,0:T(8,128)(2,1)S(1)} %subtract_convert_fusion) | copy-start | bytes 1179652
  105.2 1.1 copy-start.21
  105.2 1.1 copy-start.32
  106.3 2.9 %copy-start.2 = (f32[1,640,768]{1,2,0:T(8,128)S(1)}, f32[1,640,768]{1,2,0:T(8,128)}, u32[]{:S(2)}) copy-start(f32[1,640,768]{1,2,0:T(8,128)} %copy-done.1) | copy-start | bytes 5898244
  106.3 2.9 %copy-start.7 = (f32[1,128,768]{1,2,0:T(8,128)S(1)}, f32[1,128,768]{1,2,0:T(8,128)}, u32[]{:S(2)}) copy-start(f32[1,128,768]{1,2,0:T(8,128)} %copy-done.6) | copy-start | bytes 1179652
  106.3 3.1 %copy-start.15 = (f32[6,128,640]{2,1,0:T(8,128)S(1)}, f32[6,128,640]{2,1,0:T(8,128)}, u32[]{:S(2)}) copy-start(f32[6,128,640]{2,1,0:T(8,128)} %copy-done.14) | copy-start | bytes 5898244
  106.3 3.1 %copy-start.25 = (f32[640,6]{0,1:T(8,128)S(1)}, f32[640,6]{0,1:T(8,128)}, u32[]{:S(2)}) copy-start(f32[640,6]{0,1:T(8,128)} %copy-done.24) | copy-start | bytes 46084
  106.3 3.1 %copy-start.27 = (f32[128,6]{0,1:T(8,128)S(1)}, f32[128,6]{0,1:T(8,128)}, u32[]{:S(2)}) copy-start(f32[128,6]{0,1:T(8,128)} %copy-done.26) | copy-start | bytes 9220
  130.9 14.6 %copy-start.18 = (f32[1,128,6,128]{1,3,2,0:T(8,128)S(1)}, f32[1,128,6,128]{1,3,2,0:T(8,128)}, u32[]{:S(2)}) copy-start(f32[1,128,6,128]{1,3,2,0:T(8,128)} %get-tuple-element.47) | copy-start | bytes 1179652
  132.2 14.3 %collective-permute-start.8 = (bf16[1,128,1536]{2,1,0:T(8,128)(2,1)}, bf16[1,128,1536]{2,1,0:T(8,128)(2,1)S(1)}, u32[]{:S(2)}, u32[]{:S(2)}) collective-permute-start(bf16[1,128,1536]{2,1,0:T(8,128)(2,1)} %get-tuple-element.20), channel_id=1, source_target_pairs={{8,0},{16,8},{24,16},{32,24},{40,32},{48,40},{56,48},{64,56},{72,6... | collective-permute-start | bytes 1179656 | tf_op jit(solution)/shard_map/ppermute | solution.py:17
  134.1 17.3 %collective-permute-start.11 = (bf16[1,128,1536]{2,1,0:T(8,128)(2,1)}, bf16[1,128,1536]{2,1,0:T(8,128)(2,1)}, u32[]{:S(2)}, u32[]{:S(2)}) collective-permute-start(bf16[1,128,1536]{2,1,0:T(8,128)(2,1)} %get-tuple-element.21), channel_id=1, source_target_pairs={{0,16},{8,24},{16,32},{24,40},{32,48},{40,56},{48,64},{56,72},{64,... | collective-permute-start | bytes 1179656 | tf_op jit(solution)/shard_map/ppermute | solution.py:17
  136.8 15.9 %collective-permute-start.10 = (bf16[1,128,1536]{2,1,0:T(8,128)(2,1)}, bf16[1,128,1536]{2,1,0:T(8,128)(2,1)}, u32[]{:S(2)}, u32[]{:S(2)}) collective-permute-start(bf16[1,128,1536]{2,1,0:T(8,128)(2,1)} %get-tuple-element.22), channel_id=1, source_target_pairs={{16,0},{24,8},{32,16},{40,24},{48,32},{56,40},{64,48},{72,56},{80,... | collective-permute-start | bytes 1179656 | tf_op jit(solution)/shard_map/ppermute | solution.py:17
  143.6 13.0 %collective-permute-start.9 = (bf16[1,128,1536]{2,1,0:T(8,128)(2,1)}, bf16[1,128,1536]{2,1,0:T(8,128)(2,1)}, u32[]{:S(2)}, u32[]{:S(2)}) collective-permute-start(bf16[1,128,1536]{2,1,0:T(8,128)(2,1)} %get-tuple-element.23), channel_id=1, source_target_pairs={{0,8},{8,16},{16,24},{24,32},{32,40},{40,48},{48,56},{56,64},{64,7... | collective-permute-start | bytes 1179656 | tf_op jit(solution)/shard_map/ppermute | solution.py:17
where the time goes:
time: 160 us; the launch traced here: 159 us
  waiting for transfers between devices  43.9 us (27%)
  starting transfers between devices  40.7 us (25%)
  other arithmetic  26.4 us (16%)
  local copies, waits for them, and re-layouts  25.9 us (16%)
  matrix products  20.7 us (13%)
    ppermute x10, starting transfers between devices, passed_along(): lax.ppermute(value, axis, [(source, source + steps) for source in range(i...  34.8 us
    ppermute x10, waiting for transfers between devices, passed_along(): lax.ppermute(value, axis, [(source, source + steps) for source in range(i...  32 us
    unnamed x90, local copies, waits for them, and re-layouts  13.9 us
    ppermute x1, waiting for transfers between devices, padded(): lax.ppermute(tail, axis, [(i, (i + 1) % count) for i in range(ends)])  6.08 us
    ppermute x1, waiting for transfers between devices, padded(): lax.ppermute(head, axis, [((i + 1) % count, i) for i in range(ends)])  5.75 us
    reshape x2, local copies, waits for them, and re-layouts, merge_heads(): return values.reshape(values.shape[:-2] + (HEADS * HEAD_SIZE,))  5.73 us
    another operation x4, other arithmetic  5.71 us
    mul x2, other arithmetic, norm_back(): inverse * (grads - normed * jnp.mean(normed * grads, axis=-1, keepdims=Tr...  5.15 us
  transfers between devices with their start and end apart: 12, of which 8 were waited for; matrix products, arithmetic and copies ran while one was open for 7% of the time, Pallas kernels for 0%

commit v1 on v0

v1 whole, which is shorter than its diff:
```python
import functools

import jax
import jax.numpy as jnp
from jax import lax
from jax.experimental import pallas as pl
from jax.experimental.pallas import tpu as pltpu
from jax.sharding import PartitionSpec as P

HEADS = 6
SIZE = 128
ROWS = 128
ATT = HEADS * SIZE
MODEL = 1536
EPSILON = 1e-05
SCALE = SIZE ** (-0.5)
LOG2E = 1.4426950408889634
LN2 = 0.6931471805599453
SLOTS = 5
WINDOW = SLOTS * ROWS
CHUNKS = 3
WIDTH = ATT // CHUNKS
PER = HEADS // CHUNKS
TILE = 256
BLOCK = 32
F32 = jnp.float32
BF16 = jnp.bfloat16
MESH = pl.DeviceIdType.MESH
OWN = slice(2 * ROWS, 3 * ROWS)


def dot(a, b):
    return jnp.dot(a, b, preferred_element_type=F32)


def dot_nt(a, b):
    return lax.dot_general(a, b, (((1,), (1,)), ((), ())), preferred_element_type=F32)


def lane_mean(x):
    return jnp.sum(x, axis=-1, keepdims=True) * (1.0 / x.shape[-1])


def head_cols(h, base=0):
    return pl.ds(pl.multiple_of(h * SIZE + base, SIZE), SIZE)


def tile_cols(n, base=0):
    return pl.ds(pl.multiple_of(n * TILE + base, TILE), TILE)


def loop(count, body):
    def step(i, carry):
        body(i)
        return carry

    lax.fori_loop(0, count, step, 0)


def kernel(
    tm_count,
    site_count,
    nbr_ref,
    gain_ref,
    q_hbm,
    k_hbm,
    v_hbm,
    resid_hbm,
    wo_hbm,
    wqkv_hbm,
    grad_hbm,
    so_hbm,
    gq_hbm,
    gk_hbm,
    gv_hbm,
    gr_hbm,
    qraw,
    kraw,
    qw,
    kw,
    vw,
    dw,
    dl,
    mask,
    rq_b,
    rk_b,
    itot,
    out_f,
    dcol,
    e_w,
    et_w,
    ow,
    rw,
    gw,
    wo,
    wqkv,
    rsum,
    inv_b,
    nb,
    qf,
    kvb,
    pk,
    pkb,
    prb,
    dqb,
    dkbase,
    dvbase,
    rko,
    dkv,
    dn,
    so_v,
    gq_v,
    gk_v,
    gv_v,
    gr_v,
    load_sem,
    store_sem,
    kv_send,
    kv_recv,
    kv_relay,
    q_send,
    q_recv,
    q_relay,
    r_send,
    r_recv,
    g_send,
    g_recv,
    o_send,
    o_recv,
    p_send,
    p_recv,
    d_send,
    d_recv,
    d_relay,
):
    tm = lax.axis_index("tm")
    st = lax.axis_index("site")
    core = lax.rem(tm, 2)
    sib = tm + 1 - 2 * core
    right_chip = lax.rem(tm + 2 - core, tm_count)
    left_chip = lax.rem(tm - 1 - core + tm_count, tm_count)
    up = lax.rem(st + 1, site_count)
    down = lax.rem(st + site_count - 1, site_count)
    time_dests = ((right_chip, core), (left_chip, 3 + core), (sib, 1 + 2 * core))
    relay_from = 1 + 2 * core
    relay_to = 4 * core
    rest = (4 * core, 3 - 2 * core, 4 - 4 * core)

    loads = [
        pltpu.make_async_copy(src, dst, load_sem.at[n])
        for n, (src, dst) in enumerate(
            (
                (k_hbm.at[0], kraw),
                (q_hbm.at[0], qraw),
                (v_hbm.at[0], vw.at[OWN]),
                (resid_hbm.at[0], rw.at[OWN]),
                (grad_hbm.at[0], gw.at[OWN]),
                (wo_hbm, wo),
                (wqkv_hbm, wqkv),
            )
        )
    ]
    for copy in loads:
        copy.start()

    barrier = pltpu.get_barrier_semaphore()
    for offset in (1, 2, tm_count - 1, tm_count - 2):
        pl.semaphore_signal(
            barrier, inc=1, device_id={"tm": lax.rem(tm + offset, tm_count)}, device_id_type=MESH
        )
    for peer in (up, down):
        pl.semaphore_signal(barrier, inc=1, device_id={"site": peer}, device_id_type=MESH)

    row = lax.broadcasted_iota(jnp.int32, (ROWS, ROWS), 0)
    lane = lax.broadcasted_iota(jnp.int32, (ROWS, ROWS), 1)
    for slot in range(SLOTS):
        shard = tm + slot - 2
        valid = jnp.where((shard >= 0) & (shard < tm_count), 1.0, 0.0).astype(F32)
        if slot == 0:
            band = jnp.where(lane >= row, valid, 0.0)
        elif slot == SLOTS - 1:
            band = jnp.where(lane <= row, valid, 0.0)
        else:
            band = jnp.full((ROWS, ROWS), valid, F32)
        mask[:, slot * ROWS : (slot + 1) * ROWS] = band

    def normalise(raw, store, inverse, factor):
        def body(h):
            cols = head_cols(h)
            x = raw[:, cols].astype(F32)
            r = lax.rsqrt(lane_mean(x * x) + EPSILON)
            inverse[:, cols] = jnp.broadcast_to(r, (ROWS, SIZE))
            store[OWN, cols] = (x * (r * factor)).astype(BF16)

        loop(HEADS, body)

    loads[0].wait()
    normalise(kraw, kw, rk_b, 1.0)
    loads[1].wait()
    normalise(qraw, qw, rq_b, SCALE * LOG2E)
    pl.semaphore_wait(barrier, 6)

    def remote(src, dst, send, recv, device):
        return pltpu.make_async_remote_copy(
            src_ref=src,
            dst_ref=dst,
            send_sem=send,
            recv_sem=recv,
            device_id=device,
            device_id_type=MESH,
        )

    def slot_rows(slot, size=ROWS):
        return pl.ds(pl.multiple_of(slot * size, size), size)

    def kv_copy(kind, ch, n):
        device, slot = time_dests[n]
        cols = tile_cols(ch)
        src = kw.at[OWN, cols] if kind == 0 else v_hbm.at[0, :, cols]
        dst = (kw if kind == 0 else vw).at[slot_rows(slot), cols]
        return remote(
            src, dst, kv_send.at[kind, ch, n], kv_recv.at[kind, ch, slot], {"tm": device}
        )

    def kv_pass(kind, ch):
        cols = tile_cols(ch)
        buffer = kw if kind == 0 else vw
        return remote(
            buffer.at[slot_rows(relay_from), cols],
            buffer.at[slot_rows(relay_to), cols],
            kv_relay.at[kind, ch],
            kv_recv.at[kind, ch, relay_to],
            {"tm": sib},
        )

    def kv_arrive(kind, ch, slot):
        cols = tile_cols(ch)
        here = (kw if kind == 0 else vw).at[slot_rows(slot), cols]
        remote(here, here, kv_relay.at[kind, ch], kv_recv.at[kind, ch, slot], {"tm": sib}).wait_recv()

    def q_copy(n):
        device, slot = time_dests[n]
        return remote(
            qw.at[OWN], qw.at[slot_rows(slot)], q_send.at[n], q_recv.at[slot], {"tm": device}
        )

    def q_pass():
        return remote(
            qw.at[slot_rows(relay_from)],
            qw.at[slot_rows(relay_to)],
            q_relay.at[0],
            q_recv.at[relay_to],
            {"tm": sib},
        )

    def q_arrive(slot):
        here = qw.at[slot_rows(slot)]
        remote(here, here, q_relay.at[0], q_recv.at[slot], {"tm": sib}).wait_recv()

    def site_copy(n, src, dst, send, recv):
        return remote(
            src, dst.at[n * ROWS : (n + 1) * ROWS], send, recv, {"site": (up, down)[n]}
        )

    def out_copy(ch, n):
        cols = tile_cols(ch)
        return remote(
            ow.at[OWN, cols],
            ow.at[n * ROWS : (n + 1) * ROWS, cols],
            o_send.at[ch, n],
            o_recv.at[ch, n],
            {"site": (up, down)[n]},
        )

    def resid_copy(n):
        return site_copy(n, resid_hbm.at[0], rw, r_send.at[n], r_recv.at[n])

    def grad_copy(n):
        return site_copy(n, grad_hbm.at[0], gw, g_send.at[n], g_recv.at[n])

    def pack_copy(n):
        return site_copy(n, pkb.at[n * ROWS : (n + 1) * ROWS], prb, p_send.at[n], p_recv.at[n])

    def d_copy(kind, ch, n):
        device, slot = time_dests[n]
        cols = tile_cols(ch)
        buffer, size = ((dw, ROWS), (dl, 16))[kind]
        return remote(
            buffer.at[2 * size : 3 * size, cols],
            buffer.at[slot_rows(slot, size), cols],
            d_send.at[kind, ch, n],
            d_recv.at[kind, ch, slot],
            {"tm": device},
        )

    def d_pass(kind, ch):
        cols = tile_cols(ch)
        buffer, size = ((dw, ROWS), (dl, 16))[kind]
        return remote(
            buffer.at[slot_rows(relay_from, size), cols],
            buffer.at[slot_rows(relay_to, size), cols],
            d_relay.at[kind, ch],
            d_recv.at[kind, ch, relay_to],
            {"tm": sib},
        )

    def d_arrive(kind, ch, slot):
        cols = tile_cols(ch)
        buffer, size = ((dw, ROWS), (dl, 16))[kind]
        here = buffer.at[slot_rows(slot, size), cols]
        remote(here, here, d_relay.at[kind, ch], d_recv.at[kind, ch, slot], {"tm": sib}).wait_recv()

    for ch in range(CHUNKS):
        for n in range(3):
            for kind in range(2):
                kv_copy(kind, ch, n).start()
        if ch == 0:
            for n in range(2):
                resid_copy(n).start()
    for n in range(3):
        q_copy(n).start()
    loads[2].wait()

    def forward(ch):
        for kind in range(2):
            kv_arrive(kind, ch, relay_from)
            kv_pass(kind, ch).start()
        for slot in rest:
            for kind in range(2):
                kv_arrive(kind, ch, slot)
        for part in range(PER):
            h = ch * PER + part
            cols = head_cols(h)
            weights = (
                jnp.exp2(dot_nt(qw[OWN, cols], kw[:, cols])) * mask[...]
            ).astype(BF16)
            e_w[h] = weights
            inverse = 1.0 / jnp.sum(weights.astype(F32), axis=-1, keepdims=True)
            heads_out = dot(weights, vw[:, cols]) * inverse
            itot[:, cols] = jnp.broadcast_to(inverse, (ROWS, SIZE))
            out_f[:, cols] = heads_out
            ow[OWN, cols] = heads_out.astype(BF16)
        for n in range(2):
            out_copy(ch, n).start()

    loop(CHUNKS, forward)
    for n in range(2):
        grad_copy(n).start()

    def project_out(first, count):
        rows = slice(first, first + count)

        def body(n):
            cols = tile_cols(n)
            rsum[rows, cols] = rw[rows, cols].astype(F32) + dot(ow[rows, :], wo[:, cols])

        loop(MODEL // TILE, body)

    def norm_rows(first, count):
        def body(b):
            rows = pl.ds(pl.multiple_of(first + b * BLOCK, BLOCK), BLOCK)
            x = rsum[rows, :]
            inverse = lax.rsqrt(lane_mean(x * x) + EPSILON)
            inv_b[rows, :] = jnp.broadcast_to(inverse, (BLOCK, SIZE))
            nb[rows, :] = (x * inverse * gain_ref[...]).astype(BF16)

        loop(count // BLOCK, body)

    def project_q(first, count):
        rows = slice(first, first + count)

        def body(n):
            qf[rows, tile_cols(n)] = dot(nb[rows, :], wqkv[:, tile_cols(n)])

        loop(ATT // TILE, body)

    def project_kv(first, count):
        rows = slice(first, first + count)

        def body(n):
            kvb[rows, tile_cols(n)] = dot(nb[rows, :], wqkv[:, tile_cols(n, ATT)]).astype(BF16)

        loop(2 * ATT // TILE, body)

    loads[3].wait()
    loads[5].wait()
    project_out(2 * ROWS, ROWS)
    norm_rows(2 * ROWS, ROWS)
    loads[6].wait()
    project_q(2 * ROWS, ROWS)
    project_kv(2 * ROWS, ROWS)
    q_arrive(relay_from)
    q_pass().start()

    for n in range(2):
        resid_copy(n).wait_recv()
        for ch in range(CHUNKS):
            out_copy(ch, n).wait_recv()
    project_out(0, 2 * ROWS)
    norm_rows(0, 2 * ROWS)
    project_kv(0, 2 * ROWS)
    loads[4].wait()

    first_named, second_named = nbr_ref[0, 0], nbr_ref[0, 1]
    seen = [
        jnp.where((first_named == peer) | (second_named == peer), 1.0, 0.0).astype(F32)
        for peer in (st - 1, st + 1)
    ]

    def site_head(h):
        cols = head_cols(h)
        q = qf[OWN, cols]
        grad = gw[OWN, cols].astype(F32)
        keys = [kvb[x * ROWS : (x + 1) * ROWS, cols].astype(F32) for x in range(3)]
        values = [
            kvb[x * ROWS : (x + 1) * ROWS, head_cols(h, ATT)].astype(F32) for x in range(3)
        ]
        q_inv = lax.rsqrt(lane_mean(q * q) + EPSILON)
        k_inv = [lax.rsqrt(lane_mean(k * k) + EPSILON) for k in keys]
        scores = [
            jnp.sum(q * k, axis=-1, keepdims=True) * (q_inv * r * SCALE)
            for k, r in zip(keys, k_inv)
        ]
        exps = [jnp.exp(s) for s in scores]
        exps = [exps[0] * seen[0], exps[1] * seen[1], exps[2]]
        inverse = 1.0 / (exps[0] + exps[1] + exps[2])
        probs = [e * inverse for e in exps]
        rounded = [p.astype(BF16).astype(F32) for p in probs]
        dprobs = [jnp.sum(grad * v, axis=-1, keepdims=True) for v in values]
        delta = probs[0] * dprobs[0] + probs[1] * dprobs[1] + probs[2] * dprobs[2]
        dscores = [p * (d - delta) for p, d in zip(probs, dprobs)]
        along = [d * s for d, s in zip(dscores, scores)]
        scaled = [d * (q_inv * SCALE) for d in dscores]
        for n in range(2):
            x = 1 - n
            rows = slice(n * ROWS, (n + 1) * ROWS)
            old = pk[rows, :]
            pk[rows, :] = jnp.where(
                lane == h,
                scaled[x],
                jnp.where(lane == h + 8, along[x], jnp.where(lane == h + 16, rounded[x], old)),
            )
        so_v[:, cols] = (
            rounded[0] * values[0] + rounded[1] * values[1] + rounded[2] * values[2]
        ).astype(BF16)
        dq = (
            scaled[0] * k_inv[0] * keys[0]
            + scaled[1] * k_inv[1] * keys[1]
            + scaled[2] * k_inv[2] * keys[2]
            - q * (q_inv * q_inv * (along[0] + along[1] + along[2]) * (1.0 / SIZE))
        )
        dqb[:, cols] = dq.astype(BF16)
        dkbase[:, cols] = (scaled[2] * k_inv[2]) * q - (
            k_inv[2] * k_inv[2] * along[2] * (1.0 / SIZE)
        ) * keys[2]
        dvbase[:, cols] = rounded[2] * grad
        rko[:, cols] = jnp.broadcast_to(k_inv[2], (ROWS, SIZE))

    pk[...] = jnp.zeros_like(pk)
    loop(HEADS, site_head)
    pkb[...] = pk[...].astype(BF16)
    for n in range(2):
        pack_copy(n).start()
    so_store = pltpu.make_async_copy(so_v, so_hbm.at[0], store_sem.at[0])
    so_store.start()

    def back_q(n):
        dn[:, tile_cols(n)] = dot_nt(dqb[...], wqkv[tile_cols(n), :ATT])

    loop(MODEL // TILE, back_q)
    project_q(0, 2 * ROWS)

    for slot in rest:
        q_arrive(slot)

    def key_side(h):
        cols = head_cols(h)
        et_w[h] = (jnp.exp2(dot_nt(kw[OWN, cols], qw[:, cols])) * mask[...]).astype(BF16)

    loop(HEADS, key_side)

    for n in range(2):
        grad_copy(n).wait_recv()
        pack_copy(n).wait_recv()

    def site_keys(h):
        cols = head_cols(h)
        pick_row = lax.broadcasted_iota(jnp.int32, (SIZE, 3 * SIZE), 0)
        pick_col = lax.broadcasted_iota(jnp.int32, (SIZE, 3 * SIZE), 1)
        pick = jnp.where(pick_row == pick_col // SIZE * 8 + h, 1.0, 0.0).astype(BF16)
        spread = dot(prb[...], pick)
        inverse = rko[:, cols]
        dkey, dvalue, along = dkbase[:, cols], dvbase[:, cols], 0.0
        gathered = 0.0
        for x in range(2):
            rows = slice(x * ROWS, (x + 1) * ROWS)
            gathered = gathered + spread[rows, :SIZE] * qf[rows, cols]
            along = along + spread[rows, SIZE : 2 * SIZE]
            dvalue = dvalue + spread[rows, 2 * SIZE :] * gw[rows, cols].astype(F32)
        own_key = kvb[OWN, cols].astype(F32)
        dkey = dkey + inverse * gathered - inverse * inverse * (1.0 / SIZE) * along * own_key
        dkv[:, cols] = dkey.astype(BF16)
        dkv[:, head_cols(h, ATT)] = dvalue.astype(BF16)

    loop(HEADS, site_keys)

    def back_kv(n):
        cols = tile_cols(n)
        dn[:, cols] += dot_nt(dkv[...], wqkv[cols, ATT:])

    loop(MODEL // TILE, back_kv)

    def back_norm(b):
        rows = pl.ds(pl.multiple_of(b * BLOCK, BLOCK), BLOCK)
        own = pl.ds(pl.multiple_of(2 * ROWS + b * BLOCK, BLOCK), BLOCK)
        inverse = inv_b[own, :][:, :1]
        x = rsum[own, :]
        gained = gain_ref[...] * dn[rows, :]
        average = lane_mean(x * gained)
        gr_v[rows, :] = (
            inverse * gained - x * (inverse * inverse * inverse * average)
        ).astype(BF16)

    loop(ROWS // BLOCK, back_norm)
    gr_store = pltpu.make_async_copy(gr_v, gr_hbm.at[0], store_sem.at[1])
    gr_store.start()

    def back_out(ch):
        cols = tile_cols(ch)
        d_rows = (dot_nt(gr_v[...], wo[cols, :]) * itot[:, cols]).astype(BF16)
        dw[OWN, cols] = d_rows
        product = out_f[:, cols] * d_rows.astype(F32)
        high = product.astype(BF16)
        low = (product - high.astype(F32)).astype(BF16)
        ones = jnp.ones((16, SIZE), BF16)
        kept = lax.broadcasted_iota(jnp.int32, (16, SIZE), 0)
        for part in range(PER):
            cut = slice(part * SIZE, (part + 1) * SIZE)
            here = head_cols(ch * PER + part)
            total = jnp.sum(product[:, cut], axis=-1, keepdims=True)
            dcol[:, here] = jnp.broadcast_to(total, (ROWS, SIZE))
            line = dot_nt(ones, high[:, cut]) + dot_nt(ones, low[:, cut])
            top = line.astype(BF16).astype(F32)
            dl[32:48, here] = jnp.where(
                kept == 0, top, jnp.where(kept == 1, line - top, 0.0)
            ).astype(BF16)
        for n in range(3):
            for kind in range(2):
                d_copy(kind, ch, n).start()

    loop(CHUNKS, back_out)

    def query_side(ch):
        for part in range(PER):
            h = ch * PER + part
            cols = head_cols(h)
            dprobs = dot_nt(dw[OWN, cols], vw[:, cols])
            dscores = e_w[h].astype(F32) * (dprobs - dcol[:, cols][:, :1])
            grads = dot(dscores.astype(BF16), kw[:, cols]) * SCALE
            inverse = rq_b[:, cols]
            normed = qraw[:, cols].astype(F32) * inverse
            gq_v[:, cols] = (inverse * (grads - normed * lane_mean(normed * grads))).astype(BF16)
        for kind in range(2):
            d_arrive(kind, ch, relay_from)
            d_pass(kind, ch).start()

    loop(CHUNKS, query_side)
    gq_store = pltpu.make_async_copy(gq_v, gq_hbm.at[0], store_sem.at[2])
    gq_store.start()

    def key_grads(ch):
        for slot in rest:
            for kind in range(2):
                d_arrive(kind, ch, slot)
        for part in range(PER):
            h = ch * PER + part
            cols = head_cols(h)
            d_rows = dw[:, cols]
            lines = []
            for slot in range(SLOTS):
                line = dl[slot * 16 : (slot + 1) * 16, cols].astype(F32)
                lines.append(line[0:1] + line[1:2])
            weights = et_w[h]
            dprobs = dot_nt(vw[OWN, cols], d_rows)
            dscores = weights.astype(F32) * (dprobs - jnp.concatenate(lines, axis=1))
            grads = dot(dscores.astype(BF16), qw[:, cols]) * LN2
            inverse = rk_b[:, cols]
            normed = kraw[:, cols].astype(F32) * inverse
            gk_v[:, cols] = (inverse * (grads - normed * lane_mean(normed * grads))).astype(BF16)
            gv_v[:, cols] = dot(weights, d_rows).astype(BF16)

    loop(CHUNKS, key_grads)
    gk_store = pltpu.make_async_copy(gk_v, gk_hbm.at[0], store_sem.at[3])
    gv_store = pltpu.make_async_copy(gv_v, gv_hbm.at[0], store_sem.at[4])
    gk_store.start()
    gv_store.start()

    for ch in range(CHUNKS):
        for kind in range(2):
            for n in range(3):
                kv_copy(kind, ch, n).wait_send()
                d_copy(kind, ch, n).wait_send()
            kv_pass(kind, ch).wait_send()
            d_pass(kind, ch).wait_send()
        for n in range(2):
            out_copy(ch, n).wait_send()
    for n in range(3):
        q_copy(n).wait_send()
    q_pass().wait_send()
    for n in range(2):
        resid_copy(n).wait_send()
        grad_copy(n).wait_send()
        pack_copy(n).wait_send()
    for copy in (so_store, gr_store, gq_store, gk_store, gv_store):
        copy.wait()


def shards(tm_count, site_count, q_time, k_time, v_time, resid, w_out_time, norm_gain, w_qkv_site, grad_site, nbr_blocks):
    assert q_time.shape == (1, ROWS, ATT) and resid.shape == (1, ROWS, MODEL)
    anywhere = pl.BlockSpec(memory_space=pl.ANY)
    narrow = jax.ShapeDtypeStruct((1, ROWS, ATT), BF16)
    wide = jax.ShapeDtypeStruct((1, ROWS, MODEL), BF16)
    vmem = pltpu.VMEM
    dma = pltpu.SemaphoreType.DMA
    return pl.pallas_call(
        functools.partial(kernel, tm_count, site_count),
        out_shape=(narrow, narrow, narrow, narrow, wide),
        in_specs=[
            pl.BlockSpec(memory_space=pltpu.SMEM),
            pl.BlockSpec(memory_space=pltpu.VMEM),
        ]
        + [anywhere] * 7,
        out_specs=(anywhere,) * 5,
        scratch_shapes=[
            vmem((ROWS, ATT), BF16),
            vmem((ROWS, ATT), BF16),
            vmem((WINDOW, ATT), BF16),
            vmem((WINDOW, ATT), BF16),
            vmem((WINDOW, ATT), BF16),
            vmem((WINDOW, ATT), BF16),
            vmem((SLOTS * 16, ATT), BF16),
            vmem((ROWS, WINDOW), F32),
            vmem((ROWS, ATT), F32),
            vmem((ROWS, ATT), F32),
            vmem((ROWS, ATT), F32),
            vmem((ROWS, ATT), F32),
            vmem((ROWS, ATT), F32),
            vmem((HEADS, ROWS, WINDOW), BF16),
            vmem((HEADS, ROWS, WINDOW), BF16),
            vmem((3 * ROWS, ATT), BF16),
            vmem((3 * ROWS, MODEL), BF16),
            vmem((3 * ROWS, ATT), BF16),
            vmem((ATT, MODEL), BF16),
            vmem((MODEL, 3 * ATT), BF16),
            vmem((3 * ROWS, MODEL), F32),
            vmem((3 * ROWS, SIZE), F32),
            vmem((3 * ROWS, MODEL), BF16),
            vmem((3 * ROWS, ATT), F32),
            vmem((3 * ROWS, 2 * ATT), BF16),
            vmem((2 * ROWS, SIZE), F32),
            vmem((2 * ROWS, SIZE), BF16),
            vmem((2 * ROWS, SIZE), BF16),
            vmem((ROWS, ATT), BF16),
            vmem((ROWS, ATT), F32),
            vmem((ROWS, ATT), F32),
            vmem((ROWS, ATT), F32),
            vmem((ROWS, 2 * ATT), BF16),
            vmem((ROWS, MODEL), F32),
            vmem((ROWS, ATT), BF16),
            vmem((ROWS, ATT), BF16),
            vmem((ROWS, ATT), BF16),
            vmem((ROWS, ATT), BF16),
            vmem((ROWS, MODEL), BF16),
            dma((7,)),
            dma((5,)),
            dma((2, CHUNKS, 3)),
            dma((2, CHUNKS, SLOTS)),
            dma((2, CHUNKS)),
            dma((3,)),
            dma((SLOTS,)),
            dma((1,)),
            dma((2,)),
            dma((2,)),
            dma((2,)),
            dma((2,)),
            dma((CHUNKS, 2)),
            dma((CHUNKS, 2)),
            dma((2,)),
            dma((2,)),
            dma((2, CHUNKS, 3)),
            dma((2, CHUNKS, SLOTS)),
            dma((2, CHUNKS)),
        ],
        compiler_params=pltpu.CompilerParams(
            collective_id=0, has_side_effects=True, vmem_limit_bytes=56 * 1024 * 1024
        ),
    )(
        nbr_blocks,
        norm_gain.reshape(1, MODEL),
        q_time,
        k_time,
        v_time,
        resid,
        w_out_time,
        w_qkv_site,
        grad_site,
    )


def solution(mesh):
    rows = P("site", "tm", None)
    return jax.shard_map(
        functools.partial(shards, mesh.shape["tm"], mesh.shape["site"]),
        mesh=mesh,
        in_specs=(rows, rows, rows, rows, P(), P(), P(), rows, P("site", None)),
        out_specs=(rows,) * 5,
        check_vma=False,
    )
```

time: 160 us -> 75.6 us (0.47)
  the two profiles are of different devices: /device:TPU:24 before, /device:TPU:6 now
where the time goes in v1:
time: 75.6 us; the launch traced here: 75.3 us
  Pallas kernels  65.2 us (86%)
  local copies, waits for them, and re-layouts  9.52 us (13%)
    pallas_call x1, Pallas kernels, shards(): pl.pallas_call(functools.partial(kernel, tm_count, site_count), out_shape...  65.2 us
    unnamed x5, local copies, waits for them, and re-layouts  8.23 us

profile of v1, /device:TPU:6, one launch (start us, length us, event | category | flops | bytes accessed | tf_op | source)
XLA Modules:
  0.0 75.3 jit_solution(12635193586452566517)
XLA Ops:
  0.6 1.3 %reshape.13.gain_ref = f32[1,1536]{1,0:T(1,128)} reshape(f32[1536]{0:T(1024)} %param.14) | data formatting | bytes 12288 | tf_op jit(solution)/shard_map/reshape | solution.py:699
  1.9 65.2 %shard_map.128 = (bf16[1,128,768]{2,1,0:T(8,128)(2,1)}, bf16[1,128,768]{2,1,0:T(8,128)(2,1)}, bf16[1,128,768]{2,1,0:T(8,128)(2,1)}, bf16[1,128,768]{2,1,0:T(8,128)(2,1)}, bf16[1,128,1536]{2,1,0:T(8,128)(2,1)}) custom-call(s32[1,2]{1,0:T(1,128)} %nbr_ref.1, f32[1,1536]{1,0:T(1,128)} %reshape.13.gain_ref, bf16[1,128,768]{2,1,0:T(8,128)(2,1)} %q_hbm.1, ...), custom_call_target="tpu_custom_call" | custom-call | tf_op jit(solution)/shard_map/pallas_call | solution.py:625
  67.1 1.6 %copy.19 = bf16[1,128,768]{2,1,0:T(8,128)(2,1)} copy(bf16[1,128,768]{2,1,0:T(8,128)(2,1)} %get-tuple-element.10) | data formatting | bytes 393216
  68.7 1.6 %copy.20 = bf16[1,128,768]{2,1,0:T(8,128)(2,1)} copy(bf16[1,128,768]{2,1,0:T(8,128)(2,1)} %get-tuple-element.11) | data formatting | bytes 393216
  70.3 1.6 %copy.21 = bf16[1,128,768]{2,1,0:T(8,128)(2,1)} copy(bf16[1,128,768]{2,1,0:T(8,128)(2,1)} %get-tuple-element.12) | data formatting | bytes 393216
  71.9 1.6 %copy.22 = bf16[1,128,768]{2,1,0:T(8,128)(2,1)} copy(bf16[1,128,768]{2,1,0:T(8,128)(2,1)} %get-tuple-element.13) | data formatting | bytes 393216
  73.6 1.8 %copy.23 = bf16[1,128,1536]{2,1,0:T(8,128)(2,1)} copy(bf16[1,128,1536]{2,1,0:T(8,128)(2,1)} %get-tuple-element.14) | data formatting | bytes 786432

commit v2 on v1

--- a/solution.py
+++ b/solution.py
@@ -42,19 +42,16 @@
 
 
 def head_cols(h, base=0):
-    return pl.ds(pl.multiple_of(h * SIZE + base, SIZE), SIZE)
+    return slice(h * SIZE + base, (h + 1) * SIZE + base)
 
 
 def tile_cols(n, base=0):
-    return pl.ds(pl.multiple_of(n * TILE + base, TILE), TILE)
+    return slice(n * TILE + base, (n + 1) * TILE + base)
 
 
 def loop(count, body):
-    def step(i, carry):
+    for i in range(count):
         body(i)
-        return carry
-
-    lax.fori_loop(0, count, step, 0)
 
 
 def kernel(
@@ -99,7 +96,7 @@
     nb,
     qf,
     kvb,
-    pk,
+    pick,
     pkb,
     prb,
     dqb,
@@ -184,6 +181,10 @@
             band = jnp.full((ROWS, ROWS), valid, F32)
         mask[:, slot * ROWS : (slot + 1) * ROWS] = band
 
+    for h in range(HEADS):
+        for n in range(3):
+            pick[:, head_cols(3 * h + n)] = jnp.where(row == 8 * n + h, 1.0, 0.0).astype(BF16)
+
     def normalise(raw, store, inverse, factor):
         def body(h):
             cols = head_cols(h)
@@ -193,12 +194,6 @@
             store[OWN, cols] = (x * (r * factor)).astype(BF16)
 
         loop(HEADS, body)
-
-    loads[0].wait()
-    normalise(kraw, kw, rk_b, 1.0)
-    loads[1].wait()
-    normalise(qraw, qw, rq_b, SCALE * LOG2E)
-    pl.semaphore_wait(barrier, 6)
 
     def remote(src, dst, send, recv, device):
         return pltpu.make_async_remote_copy(
@@ -275,8 +270,15 @@
     def resid_copy(n):
         return site_copy(n, resid_hbm.at[0], rw, r_send.at[n], r_recv.at[n])
 
-    def grad_copy(n):
-        return site_copy(n, grad_hbm.at[0], gw, g_send.at[n], g_recv.at[n])
+    def grad_copy(half, n):
+        cols = slice(half * (ATT // 2), (half + 1) * (ATT // 2))
+        return remote(
+            grad_hbm.at[0, :, cols],
+            gw.at[n * ROWS : (n + 1) * ROWS, cols],
+            g_send.at[half, n],
+            g_recv.at[half, n],
+            {"site": (up, down)[n]},
+        )
 
     def pack_copy(n):
         return site_copy(n, pkb.at[n * ROWS : (n + 1) * ROWS], prb, p_send.at[n], p_recv.at[n])
@@ -284,7 +286,7 @@
     def d_copy(kind, ch, n):
         device, slot = time_dests[n]
         cols = tile_cols(ch)
-        buffer, size = ((dw, ROWS), (dl, 16))[kind]
+        buffer, size = ((dw, ROWS), (dl, 8))[kind]
         return remote(
             buffer.at[2 * size : 3 * size, cols],
             buffer.at[slot_rows(slot, size), cols],
@@ -295,7 +297,7 @@
 
     def d_pass(kind, ch):
         cols = tile_cols(ch)
-        buffer, size = ((dw, ROWS), (dl, 16))[kind]
+        buffer, size = ((dw, ROWS), (dl, 8))[kind]
         return remote(
             buffer.at[slot_rows(relay_from, size), cols],
             buffer.at[slot_rows(relay_to, size), cols],
@@ -306,23 +308,48 @@
 
     def d_arrive(kind, ch, slot):
         cols = tile_cols(ch)
-        buffer, size = ((dw, ROWS), (dl, 16))[kind]
+        buffer, size = ((dw, ROWS), (dl, 8))[kind]
         here = buffer.at[slot_rows(slot, size), cols]
         remote(here, here, d_relay.at[kind, ch], d_recv.at[kind, ch, slot], {"tm": sib}).wait_recv()
 
+    pl.semaphore_wait(barrier, 6)
+    for n in range(3):
+        kv_copy(1, 0, n).start()
+    for n in range(2):
+        resid_copy(n).start()
+    loads[0].wait()
+    normalise(kraw, kw, rk_b, 1.0)
     for ch in range(CHUNKS):
-        for n in range(3):
-            for kind in range(2):
-                kv_copy(kind, ch, n).start()
-        if ch == 0:
-            for n in range(2):
-                resid_copy(n).start()
+        for kind in range(2) if ch == 0 else (1, 0):
+            if (kind, ch) != (1, 0):
+                for n in range(3):
+                    kv_copy(kind, ch, n).start()
     for n in range(3):
+        if n == 0:
+            loads[1].wait()
+            normalise(qraw, qw, rq_b, SCALE * LOG2E)
         q_copy(n).start()
     loads[2].wait()
+    loads[3].wait()
+    loads[5].wait()
+
+    def project_out(ch, first, count):
+        rows = slice(first, first + count)
+        squares = 0.0
+        for n in range(MODEL // TILE):
+            cols = tile_cols(n)
+            before = rw[rows, cols].astype(F32) if ch == 0 else rsum[rows, cols]
+            x = before + dot(ow[rows, tile_cols(ch)], wo[tile_cols(ch), cols])
+            rsum[rows, cols] = x
+            if ch == CHUNKS - 1:
+                nb[rows, cols] = (x * gain_ref[cols][None, :]).astype(BF16)
+                squares = squares + x[:, :SIZE] * x[:, :SIZE] + x[:, SIZE:] * x[:, SIZE:]
+        if ch == CHUNKS - 1:
+            mean = jnp.sum(squares, axis=-1, keepdims=True) * (1.0 / MODEL)
+            inv_b[rows, :] = jnp.broadcast_to(lax.rsqrt(mean + EPSILON), (count, SIZE))
 
     def forward(ch):
-        for kind in range(2):
+        for kind in (1, 0):
             kv_arrive(kind, ch, relay_from)
             kv_pass(kind, ch).start()
         for slot in rest:
@@ -342,35 +369,18 @@
             ow[OWN, cols] = heads_out.astype(BF16)
         for n in range(2):
             out_copy(ch, n).start()
+        project_out(ch, 2 * ROWS, ROWS)
 
     loop(CHUNKS, forward)
     for n in range(2):
-        grad_copy(n).start()
-
-    def project_out(first, count):
-        rows = slice(first, first + count)
-
-        def body(n):
-            cols = tile_cols(n)
-            rsum[rows, cols] = rw[rows, cols].astype(F32) + dot(ow[rows, :], wo[:, cols])
-
-        loop(MODEL // TILE, body)
-
-    def norm_rows(first, count):
-        def body(b):
-            rows = pl.ds(pl.multiple_of(first + b * BLOCK, BLOCK), BLOCK)
-            x = rsum[rows, :]
-            inverse = lax.rsqrt(lane_mean(x * x) + EPSILON)
-            inv_b[rows, :] = jnp.broadcast_to(inverse, (BLOCK, SIZE))
-            nb[rows, :] = (x * inverse * gain_ref[...]).astype(BF16)
-
-        loop(count // BLOCK, body)
+        grad_copy(0, n).start()
 
     def project_q(first, count):
         rows = slice(first, first + count)
 
         def body(n):
-            qf[rows, tile_cols(n)] = dot(nb[rows, :], wqkv[:, tile_cols(n)])
+            inverse = jnp.concatenate([inv_b[rows, :]] * 2, axis=1)
+            qf[rows, tile_cols(n)] = dot(nb[rows, :], wqkv[:, tile_cols(n)]) * inverse
 
         loop(ATT // TILE, body)
 
@@ -378,27 +388,15 @@
         rows = slice(first, first + count)
 
         def body(n):
-            kvb[rows, tile_cols(n)] = dot(nb[rows, :], wqkv[:, tile_cols(n, ATT)]).astype(BF16)
+            inverse = jnp.concatenate([inv_b[rows, :]] * 2, axis=1)
+            product = dot(nb[rows, :], wqkv[:, tile_cols(n, ATT)])
+            kvb[rows, tile_cols(n)] = (product * inverse).astype(BF16)
 
         loop(2 * ATT // TILE, body)
 
-    loads[3].wait()
-    loads[5].wait()
-    project_out(2 * ROWS, ROWS)
-    norm_rows(2 * ROWS, ROWS)
     loads[6].wait()
     project_q(2 * ROWS, ROWS)
     project_kv(2 * ROWS, ROWS)
-    q_arrive(relay_from)
-    q_pass().start()
-
-    for n in range(2):
-        resid_copy(n).wait_recv()
-        for ch in range(CHUNKS):
-            out_copy(ch, n).wait_recv()
-    project_out(0, 2 * ROWS)
-    norm_rows(0, 2 * ROWS)
-    project_kv(0, 2 * ROWS)
     loads[4].wait()
 
     first_named, second_named = nbr_ref[0, 0], nbr_ref[0, 1]
@@ -407,42 +405,69 @@
         for peer in (st - 1, st + 1)
     ]
 
-    def site_head(h):
-        cols = head_cols(h)
-        q = qf[OWN, cols]
-        grad = gw[OWN, cols].astype(F32)
-        keys = [kvb[x * ROWS : (x + 1) * ROWS, cols].astype(F32) for x in range(3)]
-        values = [
-            kvb[x * ROWS : (x + 1) * ROWS, head_cols(h, ATT)].astype(F32) for x in range(3)
-        ]
+    def site_key(h, x):
+        return kvb[x * ROWS : (x + 1) * ROWS, head_cols(h)].astype(F32)
+
+    def site_value(h, x):
+        return kvb[x * ROWS : (x + 1) * ROWS, head_cols(h, ATT)].astype(F32)
+
+    def site_scores(h, x):
+        key = site_key(h, x)
+        k_inv = lax.rsqrt(lane_mean(key * key) + EPSILON)
+        score = jnp.sum(qf[OWN, head_cols(h)] * key, axis=-1, keepdims=True)
+        grad = gw[OWN, head_cols(h)].astype(F32)
+        dprob = jnp.sum(grad * site_value(h, x), axis=-1, keepdims=True)
+        return k_inv, score, dprob
+
+    own_stats = []
+    for h in range(HEADS):
+        q = qf[OWN, head_cols(h)]
         q_inv = lax.rsqrt(lane_mean(q * q) + EPSILON)
-        k_inv = [lax.rsqrt(lane_mean(k * k) + EPSILON) for k in keys]
-        scores = [
-            jnp.sum(q * k, axis=-1, keepdims=True) * (q_inv * r * SCALE)
-            for k, r in zip(keys, k_inv)
-        ]
+        own_stats.append((q_inv, site_scores(h, 2)))
+
+    q_arrive(relay_from)
+    q_pass().start()
+
+    for n in range(2):
+        resid_copy(n).wait_recv()
+    for ch in range(CHUNKS):
+        for n in range(2):
+            out_copy(ch, n).wait_recv()
+        project_out(ch, 0, 2 * ROWS)
+    project_kv(0, 2 * ROWS)
+
+    site_stats = []
+    packs = [jnp.zeros((ROWS, SIZE), F32) for _ in range(2)]
+    for h in range(HEADS):
+        q_inv, own = own_stats[h]
+        k_inv, scores, dprobs = zip(site_scores(h, 0), site_scores(h, 1), own)
+        scores = [s * (q_inv * r * SCALE) for s, r in zip(scores, k_inv)]
         exps = [jnp.exp(s) for s in scores]
         exps = [exps[0] * seen[0], exps[1] * seen[1], exps[2]]
         inverse = 1.0 / (exps[0] + exps[1] + exps[2])
         probs = [e * inverse for e in exps]
         rounded = [p.astype(BF16).astype(F32) for p in probs]
-        dprobs = [jnp.sum(grad * v, axis=-1, keepdims=True) for v in values]
         delta = probs[0] * dprobs[0] + probs[1] * dprobs[1] + probs[2] * dprobs[2]
         dscores = [p * (d - delta) for p, d in zip(probs, dprobs)]
         along = [d * s for d, s in zip(dscores, scores)]
         scaled = [d * (q_inv * SCALE) for d in dscores]
         for n in range(2):
             x = 1 - n
-            rows = slice(n * ROWS, (n + 1) * ROWS)
-            old = pk[rows, :]
-            pk[rows, :] = jnp.where(
-                lane == h,
-                scaled[x],
-                jnp.where(lane == h + 8, along[x], jnp.where(lane == h + 16, rounded[x], old)),
-            )
-        so_v[:, cols] = (
-            rounded[0] * values[0] + rounded[1] * values[1] + rounded[2] * values[2]
-        ).astype(BF16)
+            for place, value in enumerate((scaled[x], along[x], rounded[x])):
+                packs[n] = jnp.where(lane == h + 8 * place, value, packs[n])
+        site_stats.append((q_inv, k_inv, rounded, along, scaled))
+    for n in range(2):
+        pkb[n * ROWS : (n + 1) * ROWS, :] = packs[n].astype(BF16)
+        pack_copy(n).start()
+    for n in range(2):
+        grad_copy(1, n).start()
+
+    def site_head(h):
+        cols = head_cols(h)
+        q_inv, k_inv, rounded, along, scaled = site_stats[h]
+        q = qf[OWN, cols]
+        keys = [site_key(h, x) for x in range(3)]
+        values = [site_value(h, x) for x in range(3)]
         dq = (
             scaled[0] * k_inv[0] * keys[0]
             + scaled[1] * k_inv[1] * keys[1]
@@ -450,17 +475,16 @@
             - q * (q_inv * q_inv * (along[0] + along[1] + along[2]) * (1.0 / SIZE))
         )
         dqb[:, cols] = dq.astype(BF16)
+        so_v[:, cols] = (
+            rounded[0] * values[0] + rounded[1] * values[1] + rounded[2] * values[2]
+        ).astype(BF16)
         dkbase[:, cols] = (scaled[2] * k_inv[2]) * q - (
             k_inv[2] * k_inv[2] * along[2] * (1.0 / SIZE)
         ) * keys[2]
-        dvbase[:, cols] = rounded[2] * grad
+        dvbase[:, cols] = rounded[2] * gw[OWN, cols].astype(F32)
         rko[:, cols] = jnp.broadcast_to(k_inv[2], (ROWS, SIZE))
 
-    pk[...] = jnp.zeros_like(pk)
     loop(HEADS, site_head)
-    pkb[...] = pk[...].astype(BF16)
-    for n in range(2):
-        pack_copy(n).start()
     so_store = pltpu.make_async_copy(so_v, so_hbm.at[0], store_sem.at[0])
     so_store.start()
 
@@ -480,15 +504,14 @@
     loop(HEADS, key_side)
 
     for n in range(2):
-        grad_copy(n).wait_recv()
         pack_copy(n).wait_recv()
 
     def site_keys(h):
         cols = head_cols(h)
-        pick_row = lax.broadcasted_iota(jnp.int32, (SIZE, 3 * SIZE), 0)
-        pick_col = lax.broadcasted_iota(jnp.int32, (SIZE, 3 * SIZE), 1)
-        pick = jnp.where(pick_row == pick_col // SIZE * 8 + h, 1.0, 0.0).astype(BF16)
-        spread = dot(prb[...], pick)
+        if h % (HEADS // 2) == 0:
+            for n in range(2):
+                grad_copy(h // (HEADS // 2), n).wait_recv()
+        spread = dot(prb[...], pick[:, 3 * h * SIZE : 3 * (h + 1) * SIZE])
         inverse = rko[:, cols]
         dkey, dvalue, along = dkbase[:, cols], dvbase[:, cols], 0.0
         gathered = 0.0
@@ -504,24 +527,21 @@
 
     loop(HEADS, site_keys)
 
-    def back_kv(n):
+    product = 0.0
+    for n in range(MODEL // TILE):
         cols = tile_cols(n)
-        dn[:, cols] += dot_nt(dkv[...], wqkv[cols, ATT:])
-
-    loop(MODEL // TILE, back_kv)
-
-    def back_norm(b):
-        rows = pl.ds(pl.multiple_of(b * BLOCK, BLOCK), BLOCK)
-        own = pl.ds(pl.multiple_of(2 * ROWS + b * BLOCK, BLOCK), BLOCK)
-        inverse = inv_b[own, :][:, :1]
-        x = rsum[own, :]
-        gained = gain_ref[...] * dn[rows, :]
-        average = lane_mean(x * gained)
-        gr_v[rows, :] = (
-            inverse * gained - x * (inverse * inverse * inverse * average)
-        ).astype(BF16)
-
-    loop(ROWS // BLOCK, back_norm)
+        gained = gain_ref[cols][None, :] * (dn[:, cols] + dot_nt(dkv[...], wqkv[cols, ATT:]))
+        dn[:, cols] = gained
+        both = rsum[OWN, cols] * gained
+        product = product + both[:, :SIZE] + both[:, SIZE:]
+    average = jnp.sum(product, axis=-1, keepdims=True) * (1.0 / MODEL)
+    inverse = inv_b[OWN, :]
+    factor = inverse * inverse * inverse * average
+    inverse = jnp.concatenate([inverse] * 2, axis=1)
+    factor = jnp.concatenate([factor] * 2, axis=1)
+    for n in range(MODEL // TILE):
+        cols = tile_cols(n)
+        gr_v[:, cols] = (inverse * dn[:, cols] - rsum[OWN, cols] * factor).astype(BF16)
     gr_store = pltpu.make_async_copy(gr_v, gr_hbm.at[0], store_sem.at[1])
     gr_store.start()
 
@@ -532,8 +552,8 @@
         product = out_f[:, cols] * d_rows.astype(F32)
         high = product.astype(BF16)
         low = (product - high.astype(F32)).astype(BF16)
-        ones = jnp.ones((16, SIZE), BF16)
-        kept = lax.broadcasted_iota(jnp.int32, (16, SIZE), 0)
+        ones = jnp.ones((8, SIZE), BF16)
+        kept = lax.broadcasted_iota(jnp.int32, (8, SIZE), 0)
         for part in range(PER):
             cut = slice(part * SIZE, (part + 1) * SIZE)
             here = head_cols(ch * PER + part)
@@ -541,7 +561,7 @@
             dcol[:, here] = jnp.broadcast_to(total, (ROWS, SIZE))
             line = dot_nt(ones, high[:, cut]) + dot_nt(ones, low[:, cut])
             top = line.astype(BF16).astype(F32)
-            dl[32:48, here] = jnp.where(
+            dl[16:24, here] = jnp.where(
                 kept == 0, top, jnp.where(kept == 1, line - top, 0.0)
             ).astype(BF16)
         for n in range(3):
@@ -578,7 +598,7 @@
             d_rows = dw[:, cols]
             lines = []
             for slot in range(SLOTS):
-                line = dl[slot * 16 : (slot + 1) * 16, cols].astype(F32)
+                line = dl[slot * 8 : (slot + 1) * 8, cols].astype(F32)
                 lines.append(line[0:1] + line[1:2])
             weights = et_w[h]
             dprobs = dot_nt(vw[OWN, cols], d_rows)
@@ -609,9 +629,22 @@
     q_pass().wait_send()
     for n in range(2):
         resid_copy(n).wait_send()
-        grad_copy(n).wait_send()
+        grad_copy(0, n).wait_send()
+        grad_copy(1, n).wait_send()
         pack_copy(n).wait_send()
     for copy in (so_store, gr_store, gq_store, gk_store, gv_store):
+        copy.wait()
+
+
+def hand_over(*refs):
+    sems = refs[-1]
+    count = (len(refs) - 1) // 2
+    copies = [
+        pltpu.make_async_copy(refs[n], refs[count + n], sems.at[n]) for n in range(count)
+    ]
+    for copy in copies:
+        copy.start()
+    for copy in copies:
         copy.wait()
 
 
@@ -622,7 +655,7 @@
     wide = jax.ShapeDtypeStruct((1, ROWS, MODEL), BF16)
     vmem = pltpu.VMEM
     dma = pltpu.SemaphoreType.DMA
-    return pl.pallas_call(
+    results = pl.pallas_call(
         functools.partial(kernel, tm_count, site_count),
         out_shape=(narrow, narrow, narrow, narrow, wide),
         in_specs=[
@@ -638,7 +671,7 @@
             vmem((WINDOW, ATT), BF16),
             vmem((WINDOW, ATT), BF16),
             vmem((WINDOW, ATT), BF16),
-            vmem((SLOTS * 16, ATT), BF16),
+            vmem((SLOTS * 8, ATT), BF16),
             vmem((ROWS, WINDOW), F32),
             vmem((ROWS, ATT), F32),
             vmem((ROWS, ATT), F32),
@@ -657,7 +690,7 @@
             vmem((3 * ROWS, MODEL), BF16),
             vmem((3 * ROWS, ATT), F32),
             vmem((3 * ROWS, 2 * ATT), BF16),
-            vmem((2 * ROWS, SIZE), F32),
+            vmem((SIZE, 3 * ATT), BF16),
             vmem((2 * ROWS, SIZE), BF16),
             vmem((2 * ROWS, SIZE), BF16),
             vmem((ROWS, ATT), BF16),
@@ -681,8 +714,8 @@
             dma((1,)),
             dma((2,)),
             dma((2,)),
-            dma((2,)),
-            dma((2,)),
+            dma((2, 2)),
+            dma((2, 2)),
             dma((CHUNKS, 2)),
             dma((CHUNKS, 2)),
             dma((2,)),
@@ -696,7 +729,7 @@
         ),
     )(
         nbr_blocks,
-        norm_gain.reshape(1, MODEL),
+        norm_gain,
         q_time,
         k_time,
         v_time,
@@ -705,6 +738,13 @@
         w_qkv_site,
         grad_site,
     )
+    return pl.pallas_call(
+        hand_over,
+        out_shape=(narrow, narrow, narrow, narrow, wide),
+        in_specs=[anywhere] * 5,
+        out_specs=(anywhere,) * 5,
+        scratch_shapes=[dma((5,))],
+    )(*results)
 
 
 def solution(mesh):

time: 75.6 us -> 97.2 us (1.29)
  the two profiles are of different devices: /device:TPU:6 before, /device:TPU:8 now
where the time goes in v2:
time: 97.2 us; the launch traced here: 97.1 us
  Pallas kernels  96.5 us (99%)
    pallas_call x1, Pallas kernels, shards(): pl.pallas_call(functools.partial(kernel, tm_count, site_count), out_shape...  59.6 us
    pallas_call x1, Pallas kernels, shards(): pl.pallas_call(hand_over, out_shape=(narrow, narrow, narrow, narrow, wide...  36.9 us

profile of v2, /device:TPU:8, one launch (start us, length us, event | category | flops | bytes accessed | tf_op | source)
XLA Modules:
  0.0 97.1 jit_solution(8985834121737502643)
XLA Ops:
  0.6 59.6 %shard_map.128 = (bf16[1,128,768]{2,1,0:T(8,128)(2,1)}, bf16[1,128,768]{2,1,0:T(8,128)(2,1)}, bf16[1,128,768]{2,1,0:T(8,128)(2,1)}, bf16[1,128,768]{2,1,0:T(8,128)(2,1)}, bf16[1,128,1536]{2,1,0:T(8,128)(2,1)}) custom-call(s32[1,2]{1,0:T(1,128)} %nbr_ref.1, f32[1536]{0:T(1024)} %gain_ref.1, bf16[1,128,768]{2,1,0:T(8,128)(2,1)} %q_hbm.1, ...), custom_call_target="tpu_custom_call" | custom-call | tf_op jit(solution)/shard_map/pallas_call | solution.py:658
  60.2 36.9 %shard_map.129 = (bf16[1,128,768]{2,1,0:T(8,128)(2,1)}, bf16[1,128,768]{2,1,0:T(8,128)(2,1)}, bf16[1,128,768]{2,1,0:T(8,128)(2,1)}, bf16[1,128,768]{2,1,0:T(8,128)(2,1)}, bf16[1,128,1536]{2,1,0:T(8,128)(2,1)}) custom-call(bf16[1,128,768]{2,1,0:T(8,128)(2,1)} %get-tuple-element.10.refs_0_, bf16[1,128,768]{2,1,0:T(8,128)(2,1)} %get-tuple-element.11.refs_1_, ...), custom_call_target="tpu_custom_call" | custom-call | tf_op jit(solution)/shard_map/pallas_call | solution.py:741

commit v3 on v2

--- a/solution.py
+++ b/solution.py
@@ -637,14 +637,21 @@
 
 
 def hand_over(*refs):
+    count = len(refs) // 3
     sems = refs[-1]
-    count = (len(refs) - 1) // 2
-    copies = [
-        pltpu.make_async_copy(refs[n], refs[count + n], sems.at[n]) for n in range(count)
+    taken = [
+        pltpu.make_async_copy(refs[n], refs[2 * count + n], sems.at[0, n]) for n in range(count)
     ]
-    for copy in copies:
+    given = [
+        pltpu.make_async_copy(refs[2 * count + n], refs[count + n], sems.at[1, n])
+        for n in range(count)
+    ]
+    for copy in taken:
         copy.start()
-    for copy in copies:
+    for n in range(count):
+        taken[n].wait()
+        given[n].start()
+    for copy in given:
         copy.wait()
 
 
@@ -743,7 +750,8 @@
         out_shape=(narrow, narrow, narrow, narrow, wide),
         in_specs=[anywhere] * 5,
         out_specs=(anywhere,) * 5,
-        scratch_shapes=[dma((5,))],
+        scratch_shapes=[vmem(shape.shape, BF16) for shape in (narrow,) * 4 + (wide,)]
+        + [dma((2, 5))],
     )(*results)
 
 

time: 97.2 us -> 62.5 us (0.64)
  Pallas kernels: 96.5 us -> 61.8 us
    pallas_call x1, Pallas kernels: 36.9 us -> 2.18 us  [shards(): pl.pallas_call(hand_over, out_shape=(narrow, narrow, narrow, narrow, wide...]
where the time goes in v3:
time: 62.5 us; the launch traced here: 62.4 us
  Pallas kernels  61.8 us (99%)
  between operations  0.64 us (1%)
    pallas_call x1, Pallas kernels, shards(): pl.pallas_call(functools.partial(kernel, tm_count, site_count), out_shape...  59.6 us
    pallas_call x1, Pallas kernels, shards(): pl.pallas_call(hand_over, out_shape=(narrow, narrow, narrow, narrow, wide...  2.18 us

profile of v3, /device:TPU:8, one launch (start us, length us, event | category | flops | bytes accessed | tf_op | source)
XLA Modules:
  0.0 62.4 jit_solution(2951548833421911517)
XLA Ops:
  0.6 59.6 %shard_map.128 = (bf16[1,128,768]{2,1,0:T(8,128)(2,1)}, bf16[1,128,768]{2,1,0:T(8,128)(2,1)}, bf16[1,128,768]{2,1,0:T(8,128)(2,1)}, bf16[1,128,768]{2,1,0:T(8,128)(2,1)}, bf16[1,128,1536]{2,1,0:T(8,128)(2,1)}) custom-call(s32[1,2]{1,0:T(1,128)} %nbr_ref.1, f32[1536]{0:T(1024)} %gain_ref.1, bf16[1,128,768]{2,1,0:T(8,128)(2,1)} %q_hbm.1, ...), custom_call_target="tpu_custom_call" | custom-call | tf_op jit(solution)/shard_map/pallas_call | solution.py:665
  60.2 2.2 %shard_map.129 = (bf16[1,128,768]{2,1,0:T(8,128)(2,1)}, bf16[1,128,768]{2,1,0:T(8,128)(2,1)}, bf16[1,128,768]{2,1,0:T(8,128)(2,1)}, bf16[1,128,768]{2,1,0:T(8,128)(2,1)}, bf16[1,128,1536]{2,1,0:T(8,128)(2,1)}) custom-call(bf16[1,128,768]{2,1,0:T(8,128)(2,1)} %get-tuple-element.10.refs_0_, bf16[1,128,768]{2,1,0:T(8,128)(2,1)} %get-tuple-element.11.refs_1_, ...), custom_call_target="tpu_custom_call" | custom-call | tf_op jit(solution)/shard_map/pallas_call | solution.py:748

commit v4 on v2

--- a/solution.py
+++ b/solution.py
@@ -57,8 +57,8 @@
 def kernel(
     tm_count,
     site_count,
-    nbr_ref,
-    gain_ref,
+    nbr_hbm,
+    gain_hbm,
     q_hbm,
     k_hbm,
     v_hbm,
@@ -71,6 +71,8 @@
     gk_hbm,
     gv_hbm,
     gr_hbm,
+    nbr_ref,
+    gain_ref,
     qraw,
     kraw,
     qw,
@@ -91,6 +93,9 @@
     gw,
     wo,
     wqkv,
+    eye,
+    wo_t,
+    wkv_t,
     rsum,
     inv_b,
     nb,
@@ -154,6 +159,8 @@
                 (grad_hbm.at[0], gw.at[OWN]),
                 (wo_hbm, wo),
                 (wqkv_hbm, wqkv),
+                (gain_hbm, gain_ref),
+                (nbr_hbm, nbr_ref),
             )
         )
     ]
@@ -195,6 +202,19 @@
 
         loop(HEADS, body)
 
+    wide_row = lax.broadcasted_iota(jnp.int32, (TILE, TILE), 0)
+    wide_lane = lax.broadcasted_iota(jnp.int32, (TILE, TILE), 1)
+    eye[...] = jnp.where(wide_row == wide_lane, 1.0, 0.0).astype(BF16)
+
+    def transpose(source, base, target, first, last):
+        def body(n, carry):
+            rows = pl.ds(pl.multiple_of(n * TILE, TILE), TILE)
+            cols = pl.ds(pl.multiple_of(n * TILE + base, TILE), TILE)
+            target[rows, :] = dot_nt(eye[...], source[:, cols]).astype(BF16)
+            return carry
+
+        lax.fori_loop(first, last, body, 0)
+
     def remote(src, dst, send, recv, device):
         return pltpu.make_async_remote_copy(
             src_ref=src,
@@ -270,15 +290,8 @@
     def resid_copy(n):
         return site_copy(n, resid_hbm.at[0], rw, r_send.at[n], r_recv.at[n])
 
-    def grad_copy(half, n):
-        cols = slice(half * (ATT // 2), (half + 1) * (ATT // 2))
-        return remote(
-            grad_hbm.at[0, :, cols],
-            gw.at[n * ROWS : (n + 1) * ROWS, cols],
-            g_send.at[half, n],
-            g_recv.at[half, n],
-            {"site": (up, down)[n]},
-        )
+    def grad_copy(n):
+        return site_copy(n, grad_hbm.at[0], gw, g_send.at[n], g_recv.at[n])
 
     def pack_copy(n):
         return site_copy(n, pkb.at[n * ROWS : (n + 1) * ROWS], prb, p_send.at[n], p_recv.at[n])
@@ -332,6 +345,10 @@
     loads[2].wait()
     loads[3].wait()
     loads[5].wait()
+    loads[7].wait()
+    loads[8].wait()
+    transpose(wo, 0, wo_t, 0, MODEL // TILE)
+    loads[6].wait()
 
     def project_out(ch, first, count):
         rows = slice(first, first + count)
@@ -370,10 +387,12 @@
         for n in range(2):
             out_copy(ch, n).start()
         project_out(ch, 2 * ROWS, ROWS)
+        if ch < CHUNKS - 1:
+            transpose(wqkv, ATT, wkv_t, 3 * ch, 3 * ch + 3)
 
     loop(CHUNKS, forward)
     for n in range(2):
-        grad_copy(0, n).start()
+        grad_copy(n).start()
 
     def project_q(first, count):
         rows = slice(first, first + count)
@@ -394,7 +413,6 @@
 
         loop(2 * ATT // TILE, body)
 
-    loads[6].wait()
     project_q(2 * ROWS, ROWS)
     project_kv(2 * ROWS, ROWS)
     loads[4].wait()
@@ -459,8 +477,6 @@
     for n in range(2):
         pkb[n * ROWS : (n + 1) * ROWS, :] = packs[n].astype(BF16)
         pack_copy(n).start()
-    for n in range(2):
-        grad_copy(1, n).start()
 
     def site_head(h):
         cols = head_cols(h)
@@ -504,13 +520,11 @@
     loop(HEADS, key_side)
 
     for n in range(2):
+        grad_copy(n).wait_recv()
         pack_copy(n).wait_recv()
 
     def site_keys(h):
         cols = head_cols(h)
-        if h % (HEADS // 2) == 0:
-            for n in range(2):
-                grad_copy(h // (HEADS // 2), n).wait_recv()
         spread = dot(prb[...], pick[:, 3 * h * SIZE : 3 * (h + 1) * SIZE])
         inverse = rko[:, cols]
         dkey, dvalue, along = dkbase[:, cols], dvbase[:, cols], 0.0
@@ -530,7 +544,7 @@
     product = 0.0
     for n in range(MODEL // TILE):
         cols = tile_cols(n)
-        gained = gain_ref[cols][None, :] * (dn[:, cols] + dot_nt(dkv[...], wqkv[cols, ATT:]))
+        gained = gain_ref[cols][None, :] * (dn[:, cols] + dot(dkv[...], wkv_t[:, cols]))
         dn[:, cols] = gained
         both = rsum[OWN, cols] * gained
         product = product + both[:, :SIZE] + both[:, SIZE:]
@@ -547,7 +561,7 @@
 
     def back_out(ch):
         cols = tile_cols(ch)
-        d_rows = (dot_nt(gr_v[...], wo[cols, :]) * itot[:, cols]).astype(BF16)
+        d_rows = (dot(gr_v[...], wo_t[:, cols]) * itot[:, cols]).astype(BF16)
         dw[OWN, cols] = d_rows
         product = out_f[:, cols] * d_rows.astype(F32)
         high = product.astype(BF16)
@@ -629,8 +643,7 @@
     q_pass().wait_send()
     for n in range(2):
         resid_copy(n).wait_send()
-        grad_copy(0, n).wait_send()
-        grad_copy(1, n).wait_send()
+        grad_copy(n).wait_send()
         pack_copy(n).wait_send()
     for copy in (so_store, gr_store, gq_store, gk_store, gv_store):
         copy.wait()
@@ -638,7 +651,7 @@
 
 def hand_over(*refs):
     sems = refs[-1]
-    count = (len(refs) - 1) // 2
+    count = len(refs) // 2
     copies = [
         pltpu.make_async_copy(refs[n], refs[count + n], sems.at[n]) for n in range(count)
     ]
@@ -658,13 +671,11 @@
     results = pl.pallas_call(
         functools.partial(kernel, tm_count, site_count),
         out_shape=(narrow, narrow, narrow, narrow, wide),
-        in_specs=[
-            pl.BlockSpec(memory_space=pltpu.SMEM),
-            pl.BlockSpec(memory_space=pltpu.VMEM),
-        ]
-        + [anywhere] * 7,
+        in_specs=[pl.BlockSpec(memory_space=pltpu.HBM)] * 9,
         out_specs=(anywhere,) * 5,
         scratch_shapes=[
+            pltpu.SMEM((1, 2), jnp.int32),
+            vmem((MODEL,), F32),
             vmem((ROWS, ATT), BF16),
             vmem((ROWS, ATT), BF16),
             vmem((WINDOW, ATT), BF16),
@@ -685,6 +696,9 @@
             vmem((3 * ROWS, ATT), BF16),
             vmem((ATT, MODEL), BF16),
             vmem((MODEL, 3 * ATT), BF16),
+            vmem((TILE, TILE), BF16),
+            vmem((MODEL, ATT), BF16),
+            vmem((2 * ATT, MODEL), BF16),
             vmem((3 * ROWS, MODEL), F32),
             vmem((3 * ROWS, SIZE), F32),
             vmem((3 * ROWS, MODEL), BF16),
@@ -704,7 +718,7 @@
             vmem((ROWS, ATT), BF16),
             vmem((ROWS, ATT), BF16),
             vmem((ROWS, MODEL), BF16),
-            dma((7,)),
+            dma((9,)),
             dma((5,)),
             dma((2, CHUNKS, 3)),
             dma((2, CHUNKS, SLOTS)),
@@ -714,8 +728,8 @@
             dma((1,)),
             dma((2,)),
             dma((2,)),
-            dma((2, 2)),
-            dma((2, 2)),
+            dma((2,)),
+            dma((2,)),
             dma((CHUNKS, 2)),
             dma((CHUNKS, 2)),
             dma((2,)),
@@ -725,18 +739,13 @@
             dma((2, CHUNKS)),
         ],
         compiler_params=pltpu.CompilerParams(
-            collective_id=0, has_side_effects=True, vmem_limit_bytes=56 * 1024 * 1024
+            collective_id=0, has_side_effects=True, vmem_limit_bytes=48 * 1024 * 1024
         ),
     )(
-        nbr_blocks,
-        norm_gain,
-        q_time,
-        k_time,
-        v_time,
-        resid,
-        w_out_time,
-        w_qkv_site,
-        grad_site,
+        *(
+            pltpu.with_memory_space_constraint(x, pltpu.HBM)
+            for x in (nbr_blocks, norm_gain, q_time, k_time, v_time, resid, w_out_time, w_qkv_site, grad_site)
+        ),
     )
     return pl.pallas_call(
         hand_over,
@@ -744,6 +753,7 @@
         in_specs=[anywhere] * 5,
         out_specs=(anywhere,) * 5,
         scratch_shapes=[dma((5,))],
+        compiler_params=pltpu.CompilerParams(vmem_limit_bytes=1024 * 1024),
     )(*results)
 
 

time: 97.2 us -> 57.9 us (0.60)
  Pallas kernels: 96.5 us -> 57 us
    pallas_call x1, Pallas kernels: 36.9 us -> 1.05 us  [shards(): pl.pallas_call(hand_over, out_shape=(narrow, narrow, narrow, narrow, wide...]
    pallas_call x1, Pallas kernels: 59.6 us -> 56 us  [shards(): pl.pallas_call(functools.partial(kernel, tm_count, site_count), out_shape...]
where the time goes in v4:
time: 57.9 us; the launch traced here: 57.8 us
  Pallas kernels  57 us (98%)
  between operations  0.8 us (1%)
    pallas_call x1, Pallas kernels, shards(): pl.pallas_call(functools.partial(kernel, tm_count, site_count), out_shape...  56 us

profile of v4, /device:TPU:8, one launch (start us, length us, event | category | flops | bytes accessed | tf_op | source)
XLA Modules:
  0.0 57.8 jit_solution(1465591854562217535)
XLA Ops:
  0.6 56.0 %shard_map.128 = (bf16[1,128,768]{2,1,0:T(8,128)(2,1)S(1)}, bf16[1,128,768]{2,1,0:T(8,128)(2,1)S(1)}, bf16[1,128,768]{2,1,0:T(8,128)(2,1)S(1)}, bf16[1,128,768]{...) custom-call(s32[1,2]{1,0:T(1,128)} %nbr_hbm.1, f32[1536]{0:T(1024)} %gain_hbm.1, bf16[1,128,768]{2,1,0:T(8,128)(2,1)} %q_hbm.1, ...), custom_call_target="tpu_custom_call" | custom-call | tf_op jit(solution)/shard_map/pallas_call | solution.py:671
  56.6 1.1 %shard_map.129 = (bf16[1,128,768]{2,1,0:T(8,128)(2,1)}, bf16[1,128,768]{2,1,0:T(8,128)(2,1)}, bf16[1,128,768]{2,1,0:T(8,128)(2,1)}, bf16[1,128,768]{2,1,0:T(8,128)(2,1)}, bf16[1,128,1536]{2,1,0:T(8,128)(2,1)}) custom-call(bf16[1,128,768]{2,1,0:T(8,128)(2,1)S(1)} %get-tuple-element.10.refs_0_, bf16[1,128,768]{2,1,0:T(8,128)(2,1)S(1)} %get-tuple-element.11.refs_1_, ...), custom_call_target="tpu_custom_call" | custom-call | tf_op jit(solution)/shard_map/pallas_call | solution.py:750

commit v5 on v4

--- a/solution.py
+++ b/solution.py
@@ -443,9 +443,6 @@
         q_inv = lax.rsqrt(lane_mean(q * q) + EPSILON)
         own_stats.append((q_inv, site_scores(h, 2)))
 
-    q_arrive(relay_from)
-    q_pass().start()
-
     for n in range(2):
         resid_copy(n).wait_recv()
     for ch in range(CHUNKS):
@@ -477,6 +474,9 @@
     for n in range(2):
         pkb[n * ROWS : (n + 1) * ROWS, :] = packs[n].astype(BF16)
         pack_copy(n).start()
+
+    q_arrive(relay_from)
+    q_pass().start()
 
     def site_head(h):
         cols = head_cols(h)

time: 57.9 us -> 57.2 us (0.988)
  Pallas kernels: 57 us -> 56.3 us
    pallas_call x1, Pallas kernels: 56 us -> 55.2 us  [shards(): pl.pallas_call(functools.partial(kernel, tm_count, site_count), out_shape...]
where the time goes in v5:
time: 57.2 us; the launch traced here: 56.9 us
  Pallas kernels  56.3 us (98%)
  between operations  0.64 us (1%)
    pallas_call x1, Pallas kernels, shards(): pl.pallas_call(functools.partial(kernel, tm_count, site_count), out_shape...  55.2 us

profile of v5, /device:TPU:8, one launch (start us, length us, event | category | flops | bytes accessed | tf_op | source)
XLA Modules:
  0.0 56.9 jit_solution(18269239859745993000)
XLA Ops:
  0.6 55.2 %shard_map.128 = (bf16[1,128,768]{2,1,0:T(8,128)(2,1)S(1)}, bf16[1,128,768]{2,1,0:T(8,128)(2,1)S(1)}, bf16[1,128,768]{2,1,0:T(8,128)(2,1)S(1)}, bf16[1,128,768]{...) custom-call(s32[1,2]{1,0:T(1,128)} %nbr_hbm.1, f32[1536]{0:T(1024)} %gain_hbm.1, bf16[1,128,768]{2,1,0:T(8,128)(2,1)} %q_hbm.1, ...), custom_call_target="tpu_custom_call" | custom-call | tf_op jit(solution)/shard_map/pallas_call | solution.py:671
  55.9 1.1 %shard_map.129 = (bf16[1,128,768]{2,1,0:T(8,128)(2,1)}, bf16[1,128,768]{2,1,0:T(8,128)(2,1)}, bf16[1,128,768]{2,1,0:T(8,128)(2,1)}, bf16[1,128,768]{2,1,0:T(8,128)(2,1)}, bf16[1,128,1536]{2,1,0:T(8,128)(2,1)}) custom-call(bf16[1,128,768]{2,1,0:T(8,128)(2,1)S(1)} %get-tuple-element.10.refs_0_, bf16[1,128,768]{2,1,0:T(8,128)(2,1)S(1)} %get-tuple-element.11.refs_1_, ...), custom_call_target="tpu_custom_call" | custom-call | tf_op jit(solution)/shard_map/pallas_call | solution.py:750

commit v6 on v5

--- a/solution.py
+++ b/solution.py
@@ -66,11 +66,11 @@
     wo_hbm,
     wqkv_hbm,
     grad_hbm,
-    so_hbm,
-    gq_hbm,
-    gk_hbm,
-    gv_hbm,
-    gr_hbm,
+    so_out,
+    gq_out,
+    gk_out,
+    gv_out,
+    gr_out,
     nbr_ref,
     gain_ref,
     qraw,
@@ -102,6 +102,7 @@
     qf,
     kvb,
     pick,
+    pool,
     pkb,
     prb,
     dqb,
@@ -110,13 +111,7 @@
     rko,
     dkv,
     dn,
-    so_v,
-    gq_v,
-    gk_v,
-    gv_v,
-    gr_v,
     load_sem,
-    store_sem,
     kv_send,
     kv_recv,
     kv_relay,
@@ -135,6 +130,7 @@
     d_recv,
     d_relay,
 ):
+    so_v, gq_v, gk_v, gv_v, gr_v = (ref.at[0] for ref in (so_out, gq_out, gk_out, gv_out, gr_out))
     tm = lax.axis_index("tm")
     st = lax.axis_index("site")
     core = lax.rem(tm, 2)
@@ -191,6 +187,9 @@
     for h in range(HEADS):
         for n in range(3):
             pick[:, head_cols(3 * h + n)] = jnp.where(row == 8 * n + h, 1.0, 0.0).astype(BF16)
+
+    for h in range(HEADS):
+        pool[head_cols(h), :] = jnp.where(lane == h, 1.0, 0.0).astype(BF16)
 
     def normalise(raw, store, inverse, factor):
         def body(h):
@@ -429,19 +428,21 @@
     def site_value(h, x):
         return kvb[x * ROWS : (x + 1) * ROWS, head_cols(h, ATT)].astype(F32)
 
-    def site_scores(h, x):
-        key = site_key(h, x)
-        k_inv = lax.rsqrt(lane_mean(key * key) + EPSILON)
-        score = jnp.sum(qf[OWN, head_cols(h)] * key, axis=-1, keepdims=True)
-        grad = gw[OWN, head_cols(h)].astype(F32)
-        dprob = jnp.sum(grad * site_value(h, x), axis=-1, keepdims=True)
-        return k_inv, score, dprob
-
-    own_stats = []
-    for h in range(HEADS):
-        q = qf[OWN, head_cols(h)]
-        q_inv = lax.rsqrt(lane_mean(q * q) + EPSILON)
-        own_stats.append((q_inv, site_scores(h, 2)))
+    def head_sums(x):
+        high = x.astype(BF16)
+        low = (x - high.astype(F32)).astype(BF16)
+        return dot(high, pool[...]) + dot(low, pool[...])
+
+    def site_sums(rows, copies):
+        keys = kvb[rows, :ATT].astype(F32)
+        values = kvb[rows, ATT:].astype(F32)
+        queries = jnp.concatenate([qf[OWN, :]] * copies, axis=0)
+        grads = jnp.concatenate([gw[OWN, :].astype(F32)] * copies, axis=0)
+        k_inv = lax.rsqrt(head_sums(keys * keys) * (1.0 / SIZE) + EPSILON)
+        return k_inv, head_sums(queries * keys), head_sums(grads * values)
+
+    q_inv = lax.rsqrt(head_sums(qf[OWN, :] * qf[OWN, :]) * (1.0 / SIZE) + EPSILON)
+    own_sums = site_sums(OWN, 1)
 
     for n in range(2):
         resid_copy(n).wait_recv()
@@ -451,58 +452,61 @@
         project_out(ch, 0, 2 * ROWS)
     project_kv(0, 2 * ROWS)
 
-    site_stats = []
-    packs = [jnp.zeros((ROWS, SIZE), F32) for _ in range(2)]
-    for h in range(HEADS):
-        q_inv, own = own_stats[h]
-        k_inv, scores, dprobs = zip(site_scores(h, 0), site_scores(h, 1), own)
-        scores = [s * (q_inv * r * SCALE) for s, r in zip(scores, k_inv)]
-        exps = [jnp.exp(s) for s in scores]
-        exps = [exps[0] * seen[0], exps[1] * seen[1], exps[2]]
-        inverse = 1.0 / (exps[0] + exps[1] + exps[2])
-        probs = [e * inverse for e in exps]
-        rounded = [p.astype(BF16).astype(F32) for p in probs]
-        delta = probs[0] * dprobs[0] + probs[1] * dprobs[1] + probs[2] * dprobs[2]
-        dscores = [p * (d - delta) for p, d in zip(probs, dprobs)]
-        along = [d * s for d, s in zip(dscores, scores)]
-        scaled = [d * (q_inv * SCALE) for d in dscores]
-        for n in range(2):
-            x = 1 - n
-            for place, value in enumerate((scaled[x], along[x], rounded[x])):
-                packs[n] = jnp.where(lane == h + 8 * place, value, packs[n])
-        site_stats.append((q_inv, k_inv, rounded, along, scaled))
+    near_sums = site_sums(slice(0, 2 * ROWS), 2)
+    k_inv, scores, dprobs = (
+        [near[:ROWS], near[ROWS:], own] for near, own in zip(near_sums, own_sums)
+    )
+    scores = [s * (q_inv * r * SCALE) for s, r in zip(scores, k_inv)]
+    exps = [jnp.exp(s) for s in scores]
+    exps = [exps[0] * seen[0], exps[1] * seen[1], exps[2]]
+    inverse = 1.0 / (exps[0] + exps[1] + exps[2])
+    probs = [e * inverse for e in exps]
+    rounded = [p.astype(BF16).astype(F32) for p in probs]
+    delta = probs[0] * dprobs[0] + probs[1] * dprobs[1] + probs[2] * dprobs[2]
+    dscores = [p * (d - delta) for p, d in zip(probs, dprobs)]
+    along = [d * s for d, s in zip(dscores, scores)]
+    scaled = [d * (q_inv * SCALE) for d in dscores]
     for n in range(2):
-        pkb[n * ROWS : (n + 1) * ROWS, :] = packs[n].astype(BF16)
+        x = 1 - n
+        pack = 0.0
+        for place, value in enumerate((scaled[x], along[x], rounded[x])):
+            value = jnp.where(lane < HEADS, value, 0.0)
+            pack = pack + (pltpu.roll(value, 8 * place, 1) if place else value)
+        pkb[n * ROWS : (n + 1) * ROWS, :] = pack.astype(BF16)
         pack_copy(n).start()
+    by_key = [d * r for d, r in zip(scaled, k_inv)]
+    by_query = q_inv * q_inv * (along[0] + along[1] + along[2]) * (1.0 / SIZE)
+    by_own_key = k_inv[2] * k_inv[2] * along[2] * (1.0 / SIZE)
 
     q_arrive(relay_from)
     q_pass().start()
 
     def site_head(h):
         cols = head_cols(h)
-        q_inv, k_inv, rounded, along, scaled = site_stats[h]
         q = qf[OWN, cols]
         keys = [site_key(h, x) for x in range(3)]
         values = [site_value(h, x) for x in range(3)]
+
+        def of_head(compact):
+            return compact[:, h : h + 1]
+
+        weights = [of_head(w) for w in rounded]
+        factors = [of_head(f) for f in by_key]
         dq = (
-            scaled[0] * k_inv[0] * keys[0]
-            + scaled[1] * k_inv[1] * keys[1]
-            + scaled[2] * k_inv[2] * keys[2]
-            - q * (q_inv * q_inv * (along[0] + along[1] + along[2]) * (1.0 / SIZE))
+            factors[0] * keys[0]
+            + factors[1] * keys[1]
+            + factors[2] * keys[2]
+            - of_head(by_query) * q
         )
         dqb[:, cols] = dq.astype(BF16)
         so_v[:, cols] = (
-            rounded[0] * values[0] + rounded[1] * values[1] + rounded[2] * values[2]
+            weights[0] * values[0] + weights[1] * values[1] + weights[2] * values[2]
         ).astype(BF16)
-        dkbase[:, cols] = (scaled[2] * k_inv[2]) * q - (
-            k_inv[2] * k_inv[2] * along[2] * (1.0 / SIZE)
-        ) * keys[2]
-        dvbase[:, cols] = rounded[2] * gw[OWN, cols].astype(F32)
-        rko[:, cols] = jnp.broadcast_to(k_inv[2], (ROWS, SIZE))
+        dkbase[:, cols] = factors[2] * q - of_head(by_own_key) * keys[2]
+        dvbase[:, cols] = weights[2] * gw[OWN, cols].astype(F32)
+        rko[:, cols] = jnp.broadcast_to(of_head(k_inv[2]), (ROWS, SIZE))
 
     loop(HEADS, site_head)
-    so_store = pltpu.make_async_copy(so_v, so_hbm.at[0], store_sem.at[0])
-    so_store.start()
 
     def back_q(n):
         dn[:, tile_cols(n)] = dot_nt(dqb[...], wqkv[tile_cols(n), :ATT])
@@ -556,13 +560,13 @@
     for n in range(MODEL // TILE):
         cols = tile_cols(n)
         gr_v[:, cols] = (inverse * dn[:, cols] - rsum[OWN, cols] * factor).astype(BF16)
-    gr_store = pltpu.make_async_copy(gr_v, gr_hbm.at[0], store_sem.at[1])
-    gr_store.start()
 
     def back_out(ch):
         cols = tile_cols(ch)
         d_rows = (dot(gr_v[...], wo_t[:, cols]) * itot[:, cols]).astype(BF16)
         dw[OWN, cols] = d_rows
+        for n in range(3):
+            d_copy(0, ch, n).start()
         product = out_f[:, cols] * d_rows.astype(F32)
         high = product.astype(BF16)
         low = (product - high.astype(F32)).astype(BF16)
@@ -579,8 +583,7 @@
                 kept == 0, top, jnp.where(kept == 1, line - top, 0.0)
             ).astype(BF16)
         for n in range(3):
-            for kind in range(2):
-                d_copy(kind, ch, n).start()
+            d_copy(1, ch, n).start()
 
     loop(CHUNKS, back_out)
 
@@ -599,8 +602,6 @@
             d_pass(kind, ch).start()
 
     loop(CHUNKS, query_side)
-    gq_store = pltpu.make_async_copy(gq_v, gq_hbm.at[0], store_sem.at[2])
-    gq_store.start()
 
     def key_grads(ch):
         for slot in rest:
@@ -624,10 +625,6 @@
             gv_v[:, cols] = dot(weights, d_rows).astype(BF16)
 
     loop(CHUNKS, key_grads)
-    gk_store = pltpu.make_async_copy(gk_v, gk_hbm.at[0], store_sem.at[3])
-    gv_store = pltpu.make_async_copy(gv_v, gv_hbm.at[0], store_sem.at[4])
-    gk_store.start()
-    gv_store.start()
 
     for ch in range(CHUNKS):
         for kind in range(2):
@@ -645,8 +642,6 @@
         resid_copy(n).wait_send()
         grad_copy(n).wait_send()
         pack_copy(n).wait_send()
-    for copy in (so_store, gr_store, gq_store, gk_store, gv_store):
-        copy.wait()
 
 
 def hand_over(*refs):
@@ -672,7 +667,7 @@
         functools.partial(kernel, tm_count, site_count),
         out_shape=(narrow, narrow, narrow, narrow, wide),
         in_specs=[pl.BlockSpec(memory_space=pltpu.HBM)] * 9,
-        out_specs=(anywhere,) * 5,
+        out_specs=(pl.BlockSpec(memory_space=pltpu.VMEM),) * 5,
         scratch_shapes=[
             pltpu.SMEM((1, 2), jnp.int32),
             vmem((MODEL,), F32),
@@ -705,6 +700,7 @@
             vmem((3 * ROWS, ATT), F32),
             vmem((3 * ROWS, 2 * ATT), BF16),
             vmem((SIZE, 3 * ATT), BF16),
+            vmem((ATT, SIZE), BF16),
             vmem((2 * ROWS, SIZE), BF16),
             vmem((2 * ROWS, SIZE), BF16),
             vmem((ROWS, ATT), BF16),
@@ -713,13 +709,7 @@
             vmem((ROWS, ATT), F32),
             vmem((ROWS, 2 * ATT), BF16),
             vmem((ROWS, MODEL), F32),
-            vmem((ROWS, ATT), BF16),
-            vmem((ROWS, ATT), BF16),
-            vmem((ROWS, ATT), BF16),
-            vmem((ROWS, ATT), BF16),
-            vmem((ROWS, MODEL), BF16),
             dma((9,)),
-            dma((5,)),
             dma((2, CHUNKS, 3)),
             dma((2, CHUNKS, SLOTS)),
             dma((2, CHUNKS)),

time: 57.2 us -> 56.2 us (0.983)
  Pallas kernels: 56.3 us -> 55 us
    pallas_call x1, Pallas kernels: 55.2 us -> 54 us  [shards(): pl.pallas_call(functools.partial(kernel, tm_count, site_count), out_shape...]
where the time goes in v6:
time: 56.2 us; the launch traced here: 55.8 us
  Pallas kernels  55 us (98%)
  between operations  0.8 us (1%)
    pallas_call x1, Pallas kernels, shards(): pl.pallas_call(functools.partial(kernel, tm_count, site_count), out_shape...  54 us

profile of v6, /device:TPU:8, one launch (start us, length us, event | category | flops | bytes accessed | tf_op | source)
XLA Modules:
  0.0 55.8 jit_solution(9158057402956861850)
XLA Ops:
  0.6 54.0 %shard_map.128 = (bf16[1,128,768]{2,1,0:T(8,128)(2,1)S(1)}, bf16[1,128,768]{2,1,0:T(8,128)(2,1)S(1)}, bf16[1,128,768]{2,1,0:T(8,128)(2,1)S(1)}, bf16[1,128,768]{...) custom-call(s32[1,2]{1,0:T(1,128)} %nbr_hbm.1, f32[1536]{0:T(1024)} %gain_hbm.1, bf16[1,128,768]{2,1,0:T(8,128)(2,1)} %q_hbm.1, ...), custom_call_target="tpu_custom_call" | custom-call | tf_op jit(solution)/shard_map/pallas_call | solution.py:666
  54.6 1.1 %shard_map.129 = (bf16[1,128,768]{2,1,0:T(8,128)(2,1)}, bf16[1,128,768]{2,1,0:T(8,128)(2,1)}, bf16[1,128,768]{2,1,0:T(8,128)(2,1)}, bf16[1,128,768]{2,1,0:T(8,128)(2,1)}, bf16[1,128,1536]{2,1,0:T(8,128)(2,1)}) custom-call(bf16[1,128,768]{2,1,0:T(8,128)(2,1)S(1)} %get-tuple-element.10.refs_0_, bf16[1,128,768]{2,1,0:T(8,128)(2,1)S(1)} %get-tuple-element.11.refs_1_, ...), custom_call_target="tpu_custom_call" | custom-call | tf_op jit(solution)/shard_map/pallas_call | solution.py:740

commit v7 on v6

--- a/solution.py
+++ b/solution.py
@@ -597,11 +597,14 @@
             inverse = rq_b[:, cols]
             normed = qraw[:, cols].astype(F32) * inverse
             gq_v[:, cols] = (inverse * (grads - normed * lane_mean(normed * grads))).astype(BF16)
+
+    loop(CHUNKS, query_side)
+
+    def relay_grads(ch):
         for kind in range(2):
             d_arrive(kind, ch, relay_from)
             d_pass(kind, ch).start()
 
-    loop(CHUNKS, query_side)
 
     def key_grads(ch):
         for slot in rest:
@@ -624,7 +627,13 @@
             gk_v[:, cols] = (inverse * (grads - normed * lane_mean(normed * grads))).astype(BF16)
             gv_v[:, cols] = dot(weights, d_rows).astype(BF16)
 
-    loop(CHUNKS, key_grads)
+    relay_grads(0)
+    for ch in range(1, CHUNKS):
+        relay_grads(ch)
+        if ch < CHUNKS - 1:
+            key_grads(ch - 1)
+            key_grads(ch)
+    key_grads(CHUNKS - 1)
 
     for ch in range(CHUNKS):
         for kind in range(2):

time: 56.2 us -> 58.6 us (1.043)
  the two profiles are of different devices: /device:TPU:8 before, /device:TPU:1 now
where the time goes in v7:
time: 58.6 us; the launch traced here: 58.5 us
  Pallas kernels  57.7 us (98%)
  between operations  0.8 us (1%)
    pallas_call x1, Pallas kernels, shards(): pl.pallas_call(functools.partial(kernel, tm_count, site_count), out_shape...  56.6 us

profile of v7, /device:TPU:1, one launch (start us, length us, event | category | flops | bytes accessed | tf_op | source)
XLA Modules:
  0.0 58.5 jit_solution(17916477496658643382)
XLA Ops:
  0.6 56.6 %shard_map.128 = (bf16[1,128,768]{2,1,0:T(8,128)(2,1)S(1)}, bf16[1,128,768]{2,1,0:T(8,128)(2,1)S(1)}, bf16[1,128,768]{2,1,0:T(8,128)(2,1)S(1)}, bf16[1,128,768]{...) custom-call(s32[1,2]{1,0:T(1,128)} %nbr_hbm.1, f32[1536]{0:T(1024)} %gain_hbm.1, bf16[1,128,768]{2,1,0:T(8,128)(2,1)} %q_hbm.1, ...), custom_call_target="tpu_custom_call" | custom-call | tf_op jit(solution)/shard_map/pallas_call | solution.py:675
  57.3 1.1 %shard_map.129 = (bf16[1,128,768]{2,1,0:T(8,128)(2,1)}, bf16[1,128,768]{2,1,0:T(8,128)(2,1)}, bf16[1,128,768]{2,1,0:T(8,128)(2,1)}, bf16[1,128,768]{2,1,0:T(8,128)(2,1)}, bf16[1,128,1536]{2,1,0:T(8,128)(2,1)}) custom-call(bf16[1,128,768]{2,1,0:T(8,128)(2,1)S(1)} %get-tuple-element.10.refs_0_, bf16[1,128,768]{2,1,0:T(8,128)(2,1)S(1)} %get-tuple-element.11.refs_1_, ...), custom_call_target="tpu_custom_call" | custom-call | tf_op jit(solution)/shard_map/pallas_call | solution.py:749
